TPU v7x, 256 devices: a whole 4x4x8 slice. The times are simulated.
256 devices in a mesh: seq: 32 (over z, x), head: 8 (over y, core).
Axes of the slice: x: 4, y: 4, z: 8, core: 2. Of those that a mesh axis runs over, the one named last changes fastest.
Arguments:
- block_input: bfloat16 [8, 256, 5120], P(None, 'seq'), may hold values from -6 to 6
- accepted: bfloat16 [8, 256, 5120], P(None, 'seq'), may hold values from -6 to 6
- accept_mask: int32 [8, 256], P(None, 'seq'), may hold values 0 or 1
- cache_lengths: int32 [8], replicated, may hold values from 1 to 8192, as said below
- page_table: int32 [512], replicated, may hold values from 0 to 511, each once
- norm_gain: float32 [5120], replicated, may hold values from 0.1 to 1.9
- w_query: bfloat16 [5120, 3072], P('seq', 'head'), may hold values from -0.078125 to 0.078125
- w_key: bfloat16 [5120, 3072], P('seq', 'head'), may hold values from -0.078125 to 0.078125
- w_value: bfloat16 [5120, 3072], P('seq', 'head'), may hold values from -0.25 to 0.25
- w_out: bfloat16 [5120, 3072], P('seq', 'head'), may hold values from -0.109375 to 0.109375
- key_cache: bfloat16 [512, 128, 3072], P('seq', None, 'head')
- value_cache: bfloat16 [512, 128, 3072], P('seq', None, 'head'), may hold values from -18 to 18
Outputs:
- first_out: bfloat16 [8, 256, 5120], P(None, 'seq', 'head')
- second_out: bfloat16 [8, 256, 5120], P(None, 'seq', 'head')
Inputs may be any that keep to these rules, and one draw needn't show every extreme that they name: `cache_lengths`: max(1, 4) requests, chosen at random, hold (63) * 128 + 1 to 8192 cached tokens, one of them exactly 8192; the others hold 1 to 256. `page_table`: A permutation of the 512 pool pages; entry r * 64 + j is the pool page of cached positions j * 128 to (j + 1) * 128 - 1 of request r.
All inputs are finite; a program needn't handle non-finite values. No bound on the sum of `accept_mask` on one device may be relied on, other than what follows from the above.
Results may differ from a plain program's by a relative error of at most 0.024.
The roundings to bfloat16 on the way count: a program that leaves them out, or rounds other values in their place, can miss the bound.
Values may be sent and summed in bfloat16 or wider, within the bound.
A program may use at most 128 MiB of HBM per device.

v0:
```python
import jax
import jax.numpy as jnp
from jax import lax
from jax.sharding import PartitionSpec as P

HD = 128
PAGE = 128
MAXP = 64


masked_score = -1e30


def rotate(vectors, positions):
    half_width = vectors.shape[-1] // 2
    frequency = 10000.0 ** (-(jnp.arange(half_width).astype(jnp.float32) * 2.0) / vectors.shape[-1])
    angles = positions[..., None, None] * frequency
    cosine = jnp.cos(angles)
    sine_part = jnp.sin(angles)
    front_half = vectors[..., :half_width]
    back_half = vectors[..., half_width:]
    return jnp.concatenate(
        [front_half * cosine - back_half * sine_part, back_half * cosine + front_half * sine_part],
        axis=-1,
    )


def normalize(inputs, norm_gain):
    widened = inputs.astype(jnp.float32)
    inverse = lax.rsqrt(jnp.mean(widened * widened, axis=-1, keepdims=True) + 1e-05)
    return (widened * inverse * norm_gain).astype(jnp.bfloat16)


def per_device(
    block_input,
    accepted,
    accept_mask,
    cache_lengths,
    page_table,
    norm_gain,
    w_query,
    w_key,
    w_value,
    w_out,
    key_cache,
    value_cache,
):
    seq_place = lax.axis_index("seq")
    requests, part_len, model_width = block_input.shape
    local_width = w_query.shape[1]
    local_heads = local_width // HD
    row_count = 2 * requests * part_len
    swapped = jnp.where(accept_mask[:, :, None] == 1, accepted, block_input)
    token_rows = normalize(jnp.stack([block_input, swapped]), norm_gain).reshape(
        row_count, model_width
    )
    full_query, full_key, full_value, out_weight = (
        lax.all_gather(w_query, "seq", axis=0, tiled=True),
        lax.all_gather(w_key, "seq", axis=0, tiled=True),
        lax.all_gather(w_value, "seq", axis=0, tiled=True),
        lax.all_gather(w_out, "seq", axis=0, tiled=True),
    )
    query_rows = jnp.dot(token_rows, full_query, preferred_element_type=jnp.float32)
    key_rows = jnp.dot(token_rows, full_key, preferred_element_type=jnp.float32)
    value_rows = jnp.dot(token_rows, full_value, preferred_element_type=jnp.float32)
    positions = (
        cache_lengths[:, None]
        + seq_place * part_len
        + jnp.arange(part_len, dtype=jnp.int32)[None, :]
    ).astype(jnp.float32)
    shaped = (2, requests, part_len, local_heads, HD)
    new_queries = rotate(query_rows.reshape(shaped), positions).astype(jnp.bfloat16)
    new_keys = rotate(key_rows.reshape(shaped), positions).astype(jnp.bfloat16)
    new_values = value_rows.reshape(shaped).astype(jnp.bfloat16)
    every_query = lax.all_gather(new_queries, "seq", axis=2, tiled=True)
    pages_here = key_cache.shape[0]
    page_ids = seq_place * pages_here + jnp.arange(pages_here, dtype=jnp.int32)
    table_slots = jnp.arange(page_table.shape[0], dtype=jnp.int32)
    slot_of = jnp.sum(
        jnp.where(page_table[None, :] == page_ids[:, None], table_slots[None, :], 0), axis=1
    )
    page_owner = slot_of // MAXP
    owner_match = page_owner[:, None] == jnp.arange(requests, dtype=jnp.int32)[None, :]
    owner_length = jnp.sum(jnp.where(owner_match, cache_lengths[None, :], 0), axis=1)
    offsets = (slot_of % MAXP)[:, None] * PAGE + jnp.arange(PAGE, dtype=jnp.int32)[None, :]
    live_mask = (offsets < owner_length[:, None])[:, None, None, :]
    owner_hot = owner_match.astype(jnp.float32)
    cached_keys = key_cache.reshape(pages_here, PAGE, local_heads, HD)
    cached_values = value_cache.reshape(pages_here, PAGE, local_heads, HD)
    score_scale = HD ** (-0.5)

    def local_part(pass_items):
        pass_queries, pass_keys, pass_values = pass_items
        page_queries = jnp.take(pass_queries, page_owner, axis=0)
        scores = (
            jnp.einsum(
                "pqhd,pkhd->pqhk", page_queries, cached_keys, preferred_element_type=jnp.float32
            )
            * score_scale
        )
        scores = jnp.where(live_mask, scores, masked_score)
        page_peak = jnp.max(scores, axis=-1)
        weights = jnp.where(live_mask, jnp.exp(scores - page_peak[..., None]), 0.0)
        page_total = jnp.sum(weights, axis=-1)
        page_out = jnp.einsum(
            "pqhk,pkhd->pqhd",
            weights.astype(jnp.bfloat16),
            cached_values,
            preferred_element_type=jnp.float32,
        )
        owner_peak = jnp.max(
            jnp.where(owner_match[:, :, None, None], page_peak[:, None], masked_score), axis=0
        )
        factor = jnp.exp(page_peak - jnp.take(owner_peak, page_owner, axis=0))
        cache_total = jnp.einsum(
            "pr,pqh->rqh", owner_hot, page_total * factor, precision=lax.Precision.HIGHEST
        )
        cache_out = jnp.einsum(
            "pr,pqhd->rqhd",
            owner_hot,
            page_out * factor[..., None],
            precision=lax.Precision.HIGHEST,
        )
        block_scores = (
            jnp.einsum(
                "rqhd,rkhd->rqhk", pass_queries, pass_keys, preferred_element_type=jnp.float32
            )
            * score_scale
        )
        block_peak = jnp.max(block_scores, axis=-1)
        block_weights = jnp.exp(block_scores - block_peak[..., None])
        block_total = jnp.sum(block_weights, axis=-1)
        block_out = jnp.einsum(
            "rqhk,rkhd->rqhd",
            block_weights,
            pass_values.astype(jnp.float32),
            precision=lax.Precision.HIGHEST,
        )
        row_peak = jnp.maximum(owner_peak, block_peak)
        cache_factor = jnp.exp(owner_peak - row_peak)
        block_factor = jnp.exp(block_peak - row_peak)
        joined_total = cache_total * cache_factor + block_total * block_factor
        joined_out = cache_out * cache_factor[..., None] + block_out * block_factor[..., None]
        return (row_peak, joined_total, joined_out)

    row_peak, row_total, row_out = lax.map(local_part, (every_query, new_keys, new_values))
    overall = lax.pmax(row_peak, "seq")
    rescale = jnp.exp(row_peak - overall)
    summed_out, summed_total = (
        lax.psum_scatter(row_out * rescale[..., None], "seq", scatter_dimension=2, tiled=True),
        lax.psum_scatter(row_total * rescale, "seq", scatter_dimension=2, tiled=True),
    )
    context = (
        (summed_out / summed_total[..., None]).astype(jnp.bfloat16).reshape(row_count, local_width)
    )
    partial_value = lax.dot_general(
        context, out_weight, (((1,), (1,)), ((), ())), preferred_element_type=jnp.float32
    )
    own_share = lax.psum_scatter(partial_value, "head", scatter_dimension=1, tiled=True).astype(
        jnp.bfloat16
    )
    result = own_share.reshape(2, requests, part_len, own_share.shape[1])
    return (result[0], result[1])


def solution(mesh):
    placed = (
        P(None, "seq", None),
        P(None, "seq", None),
        P(None, "seq"),
        P(),
        P(),
        P(),
        P("seq", "head"),
        P("seq", "head"),
        P("seq", "head"),
        P("seq", "head"),
        P("seq", None, "head"),
        P("seq", None, "head"),
    )
    return jax.shard_map(
        per_device,
        mesh=mesh,
        in_specs=placed,
        out_specs=(P(None, "seq", "head"), P(None, "seq", "head")),
        check_vma=False,
    )
```

profile of v0, /device:TPU:33, one launch (start us, length us, event | category | flops | bytes accessed | tf_op | source)
XLA Modules:
  0.0 916.0 jit_solution(8133665721481068145)
XLA Ops:
  13.3 77.4 %all-gather.10.cloned.1.call-done = bf16[5120,384]{1,0:T(8,128)(2,1)} async-done(((bf16[160,384]{1,0:T(8,128)(2,1)}), bf16[5120,384]{1,0:T(8,128)(2,1)}) %all-gather.10.cloned.1.call-update) | async-done | bytes 3932176 | tf_op jit(solution)/shard_map/all_gather | solution.py:59
  90.7 6.3 copy.77
  97.0 74.6 %all-gather.6.cloned.1.call-done = bf16[5120,384]{1,0:T(8,128)(2,1)} async-done(((bf16[160,384]{1,0:T(8,128)(2,1)}), bf16[5120,384]{1,0:T(8,128)(2,1)}) %all-gather.6.cloned.1.call-update) | async-done | bytes 3932176 | tf_op jit(solution)/shard_map/all_gather | solution.py:58
  171.6 6.3 copy.75
  178.0 3.5 fusion.59
  191.2 61.3 %all-gather.12.cloned.1.call-done = bf16[5120,384]{1,0:T(8,128)(2,1)} async-done(((bf16[160,384]{1,0:T(8,128)(2,1)}), bf16[5120,384]{1,0:T(8,128)(2,1)}) %all-gather.12.cloned.1.call-update) | async-done | bytes 3932176 | tf_op jit(solution)/shard_map/all_gather | solution.py:60
  252.5 6.3 copy.79
  259.5 4.0 convolution_convert_fusion
  263.5 66.8 %all-gather.8.cloned.1.call-done = bf16[2,8,256,3,128]{4,2,3,1,0:T(8,128)(2,1)} async-done(((bf16[2,8,8,3,128]{4,2,3,1,0:T(8,128)(2,1)}), bf16[2,8,256,3,128]{4,2,3,1,0:T(8,128)(2,1)}) %all-gather.8.cloned.1.call-update) | async-done | bytes 3145744 | tf_op jit(solution)/shard_map/all_gather | solution.py:75
  330.4 82.3 %while.16 = (s32[]{:T(128)}, f32[2,8,256,3]{2,1,3,0:T(8,128)}, f32[2,8,256,3]{2,1,3,0:T(8,128)}, f32[2,8,256,3,128]{4,2,3,1,0:T(8,128)}, s32[16]{0:T(128)S(1)}, ...) while((s32[]{:T(128)}, f32[2,8,256,3]{2,1,3,0:T(8,128)}, ...), condition=%wide.region_9.10_spmd.clone.clone, body=%wide.region_3.9_spmd.clone.clone.sunk | while | flops 1071998720 | bytes 124305208 | solution.py:146
  331.9 2.7 gather_fusion
  334.7 3.0 bitcast_reduce_fusion.2
  337.7 2.2 fusion.98
  341.7 8.2 bitcast_multiply_fusion.4
  352.5 2.2 fusion.102
  354.8 2.3 copy.126
  357.1 11.2 %fusion.103 = f32[1,8,256,3,128]{4,1,3,2,0:T(8,128)S(1)} fusion(f32[8,3,128,256]{2,0,1,3:T(8,128)} %copy.126, f32[16,256,3,128]{3,1,2,0:T(8,128)} %bitcast_multiply_fusion.4, f32[8,256,3]{0,2,1:T(4,128)} %copy.127, f32[8,256,3]{0,2,1:T(4,128)} %copy.128, s32[16]{0:T(128)S(1)} %get-tuple-element.340), kind=kOutput, calls=%fused_computation.19.clone.1 | convolution fusion | flops 153354496 | bytes 12632128 | tf_op jit(solution)/shard_map/while/body/eval_jaxpr/pr,pqhd->rqhd/dot_general | solution.py:118
  373.0 2.7 gather_fusion
  375.8 3.0 bitcast_reduce_fusion.2
  378.8 2.2 fusion.98
  382.8 8.2 bitcast_multiply_fusion.4
  393.6 2.2 fusion.102
  395.9 2.3 copy.126
  398.2 11.2 %fusion.103 = f32[1,8,256,3,128]{4,1,3,2,0:T(8,128)S(1)} fusion(f32[8,3,128,256]{2,0,1,3:T(8,128)} %copy.126, f32[16,256,3,128]{3,1,2,0:T(8,128)} %bitcast_multiply_fusion.4, f32[8,256,3]{0,2,1:T(4,128)} %copy.127, f32[8,256,3]{0,2,1:T(4,128)} %copy.128, s32[16]{0:T(128)S(1)} %get-tuple-element.340), kind=kOutput, calls=%fused_computation.19.clone.1 | convolution fusion | flops 153354496 | bytes 12632128 | tf_op jit(solution)/shard_map/while/body/eval_jaxpr/pr,pqhd->rqhd/dot_general | solution.py:118
  409.5 2.3 copy_dynamic-update-slice_fusion.2
  412.7 109.3 %pmax.7 = f32[2,8,256,3]{2,1,3,0:T(8,128)S(1)} all-reduce(f32[2,8,256,3]{2,1,3,0:T(8,128)} %get-tuple-element.72), channel_id=1, replica_groups=mesh['seq'=32,'head'=8] {'seq'}, use_global_device_ids=true, to_apply=%region_10.11 | all-reduce | flops 12288 | bytes 98304 | tf_op jit(solution)/shard_map/pmax | solution.py:147
  522.9 7.3 broadcast_multiply_fusion
  532.1 111.8 %all-reduce = f32[2,8,256,3]{2,1,3,0:T(8,128)S(1)} all-reduce(f32[2,8,256,3]{2,1,3,0:T(8,128)S(1)} %get-tuple-element.201), channel_id=3, replica_groups=mesh['seq'=32,'head'=8] {'seq'}, use_global_device_ids=true, to_apply=%region_12.13.clone | all-reduce | flops 12288 | bytes 98304
  644.0 139.5 %reduce-scatter.4.cloned.1.call-done = f32[2,8,8,3,128]{4,2,3,1,0:T(8,128)} async-done(((f32[2,8,256,3,128]{4,2,3,1,0:T(8,128)}), f32[2,8,8,3,128]{4,2,3,1,0:T(8,128)}) %reduce-scatter.4.cloned.1.call-update) | async-done | bytes 196624 | tf_op jit(solution)/shard_map/reduce_scatter | solution.py:150
  784.6 82.5 %all-gather.14.cloned.1.call-done = bf16[5120,384]{1,0:T(8,128)(2,1)} async-done(((bf16[160,384]{1,0:T(8,128)(2,1)}), bf16[5120,384]{1,0:T(8,128)(2,1)}) %all-gather.14.cloned.1.call-update) | async-done | bytes 3932176 | tf_op jit(solution)/shard_map/all_gather | solution.py:61
  867.2 5.0 fusion.66
  872.2 35.3 %reduce-scatter.6.cloned.1.call-done = f32[128,640]{1,0:T(8,128)} async-done(((f32[128,5120]{1,0:T(8,128)}), f32[128,640]{1,0:T(8,128)}) %reduce-scatter.6.cloned.1.call-update) | async-done | bytes 327696 | tf_op jit(solution)/shard_map/reduce_scatter | solution.py:159
  (128 shorter events, 37.3 us)
Async XLA Ops:
  7.2 5.8 copy-start.13
  7.2 83.6 %all-gather.10.cloned.1.call-start = ((), (), s32[]{:S(2)}) async-start(), calls=%async_computation.4 | async-start | bytes 4055040 | tf_op jit(solution)/shard_map/all_gather | solution.py:59
  7.9 163.7 %all-gather.6.cloned.1.call-start = ((), (), s32[]{:S(2)}) async-start(), calls=%async_computation.2 | async-start | bytes 4055040 | tf_op jit(solution)/shard_map/all_gather | solution.py:58
  8.7 243.8 %all-gather.12.cloned.1.call-start = ((), (), s32[]{:S(2)}) async-start(), calls=%async_computation.5 | async-start | bytes 4055040 | tf_op jit(solution)/shard_map/all_gather | solution.py:60
  9.4 321.0 %all-gather.8.cloned.1.call-start = ((), (), s32[]{:S(2)}) async-start(), calls=%async_computation.3 | async-start | bytes 3244032 | tf_op jit(solution)/shard_map/all_gather | solution.py:75
  171.6 6.3 copy-start.3
  171.6 6.3 copy-start.12
  177.9 3.6 copy-start.2
  183.7 599.8 %reduce-scatter.4.cloned.1.call-start = ((), (), s32[]{:S(2)}) async-start(), calls=%async_computation.6 | async-start | bytes 6488064 | tf_op jit(solution)/shard_map/reduce_scatter | solution.py:150
  187.3 3.6 copy-start.11
  331.9 2.8 copy-start.4
  337.7 2.6 copy-start
  340.3 1.4 copy-start.5
  341.7 8.3 copy-start.1
  341.7 8.3 copy-start.6
  368.3 2.3 copy-start.9
  368.3 2.5 copy-start.7
  370.8 0.6 copy-start.10
  370.9 0.6 copy-start.8
  373.0 2.8 copy-start.4
  378.8 2.6 copy-start
  381.4 1.4 copy-start.5
  382.8 8.2 copy-start.1
  382.8 8.2 copy-start.6
  409.4 2.4 copy-start.9
  409.4 2.6 copy-start.7
  412.0 0.6 copy-start.10
  412.0 0.6 copy-start.8
  530.2 0.7 copy-start.14
  530.2 336.9 %all-gather.14.cloned.1.call-start = ((), (), s32[]{:S(2)}) async-start(), calls=%async_computation.7 | async-start | bytes 4055040 | tf_op jit(solution)/shard_map/all_gather | solution.py:61
  530.8 376.6 %reduce-scatter.6.cloned.1.call-start = ((), (), s32[]{:S(2)}) async-start(), calls=%async_computation.8 | async-start | bytes 2949120 | tf_op jit(solution)/shard_map/reduce_scatter | solution.py:159
Sparse Core Ops, SparseCore 0:
  10.6 80.1 all-gather.9
  93.3 78.2 all-gather.5
  174.2 78.2 all-gather.11
  254.8 75.4 all-gather.7
  530.3 253.1 reduce-scatter.3
  786.3 80.7 all-gather.13
  872.3 35.1 reduce-scatter.5
where the time goes:
time: 920 us; the launch traced here: 916 us
  waiting for transfers between devices  540 us (59%)
  blocking collectives  221 us (24%)
  matrix products  64.6 us (7%)
  local copies, waits for them, and re-layouts  53.1 us (6%)
  other arithmetic  21.4 us (2%)
  between operations  14.9 us (2%)
    reduce_scatter x1, waiting for transfers between devices, per_device(): lax.psum_scatter(row_out * rescale[..., None], 'seq', scatter_dimension=2...  140 us
    unnamed x1, blocking collectives  112 us
    pmax x1, blocking collectives, per_device(): overall = lax.pmax(row_peak, 'seq')  109 us
    all_gather x1, waiting for transfers between devices, per_device(): lax.all_gather(w_out, 'seq', axis=0, tiled=True)  82.5 us
    all_gather x1, waiting for transfers between devices, per_device(): lax.all_gather(w_key, 'seq', axis=0, tiled=True)  77.4 us
    all_gather x1, waiting for transfers between devices, per_device(): lax.all_gather(w_query, 'seq', axis=0, tiled=True)  74.6 us
    all_gather x1, waiting for transfers between devices, per_device(): every_query = lax.all_gather(new_queries, 'seq', axis=2, tiled=True)  66.8 us
    all_gather x1, waiting for transfers between devices, per_device(): lax.all_gather(w_value, 'seq', axis=0, tiled=True)  61.3 us
  transfers between devices with their start and end apart: 7, of which 7 were waited for; matrix products, arithmetic and copies ran while one was open for 5% of the time, Pallas kernels for 0%

commit v1 on v0

v1 whole, which is shorter than its diff:
```python
import functools

import jax
import jax.numpy as jnp
from jax import lax
from jax.experimental import pallas as pl
from jax.experimental.pallas import tpu as pltpu
from jax.sharding import PartitionSpec as P

HD = 128
PAGE = 128
MAXP = 64
X = 4
BLK = 160
COVER = 256
MESH = pl.DeviceIdType.MESH
F32 = jnp.float32
BF16 = jnp.bfloat16
NT = (((1,), (1,)), ((), ()))
TN = (((0,), (0,)), ((), ()))


def place(Z):
    seq = lax.axis_index("seq")
    head = lax.axis_index("head")
    z, x = seq // X, lax.rem(seq, X)

    def at(dz, dx):
        return (lax.rem(z + dz + Z, Z) * X + lax.rem(x + dx, X), head)

    return seq, head, z, x, at


def greet(partners):
    barrier = pltpu.get_barrier_semaphore()
    for partner in partners:
        pl.semaphore_signal(barrier, inc=1, device_id=partner, device_id_type=MESH)
    pl.semaphore_wait(barrier, len(partners))


def remote(src, dst, send, recv, target):
    return pltpu.make_async_remote_copy(
        src_ref=src, dst_ref=dst, send_sem=send, recv_sem=recv, device_id=target, device_id_type=MESH
    )


def project_kernel(
    Z,
    x_ref,
    a_ref,
    mask_ref,
    gain_ref,
    cos_ref,
    sin_ref,
    wq_ref,
    wk_ref,
    wv_ref,
    wo_ref,
    q_all,
    kn_ref,
    vn_ref,
    wo_all,
    xn,
    xg,
    wb,
    acc,
    part,
    got,
    qloc,
    ring_send,
    ring_recv,
    tok_send,
    tok_recv,
    part_send,
    part_recv,
    zq_send,
    zq_recv,
    xq_send,
    xq_recv,
    local_sem,
):
    seq, head, z, x, at = place(Z)
    width = X * BLK
    off = pl.multiple_of(32 * x, 32)
    own = (wq_ref, wk_ref, wv_ref, wo_ref)
    greet([at(d, 0) for d in range(1, Z)] + [at(0, d) for d in range(1, X)])

    def ring(right, t, k):
        block = lax.rem(z - k + Z, Z) if right else lax.rem(z + k, Z)
        slot = wo_all.at[block] if t == 3 else wb.at[t, block, pl.ds(off, BLK)]
        src = own[t] if k == 0 else slot
        way = 1 if right else 0
        return remote(
            src, slot, ring_send.at[way, t, k], ring_recv.at[way, t, k], at(1 if right else -1, 0)
        )

    def steps(t, right):
        return Z // 2 if right == (t % 2 == 0) else Z - 1 - Z // 2

    def advance(tensors, k):
        for t in tensors:
            for right in (True, False):
                if 0 < k <= steps(t, right):
                    ring(right, t, k - 1).wait_recv()
                if k < steps(t, right):
                    ring(right, t, k).start()

    advance((0, 1), 0)
    own_out = pltpu.make_async_copy(wo_ref, wo_all.at[z], local_sem.at[0])
    own_out.start()

    @pl.loop(0, x_ref.shape[0])
    def _(r):
        first = x_ref[r].astype(F32)
        second = jnp.where(mask_ref[r] == 1, a_ref[r].astype(F32), first)
        both = jnp.concatenate([first, second], axis=0)
        inverse = lax.rsqrt(jnp.mean(both * both, axis=-1, keepdims=True) + 1e-05)
        normed = (both * inverse * gain_ref[...]).astype(BF16)
        rows = pl.ds(pl.multiple_of(r * 16, 16), 16)
        for c in range(Z):
            xn[c, rows, :] = normed[:, c * width : (c + 1) * width]

    mine = pl.ds(pl.multiple_of(x * 128, 128), 128)
    tokens = []
    for d in range(1, X):
        there = lax.rem(x + d, X)
        copy = remote(
            xn.at[:, :, pl.ds(pl.multiple_of(there * 128, 128), COVER)],
            xg.at[:, mine],
            tok_send.at[d - 1],
            tok_recv.at[d - 1],
            at(0, d),
        )
        copy.start()
        tokens.append(copy)
    own_tokens = pltpu.make_async_copy(xn.at[:, :, pl.ds(pl.multiple_of(x * 128, 128), COVER)], xg.at[:, mine], local_sem.at[1])
    own_tokens.start()

    advance((0, 1), 1)

    zero = jnp.zeros((32, wb.shape[3]), BF16)

    @pl.loop(0, Z)
    def _(c):
        for t in range(3):
            for j in range(3):
                stripe = pl.multiple_of(32 * lax.rem(x + 5 + j, 8), 32)
                wb[t, c, pl.ds(stripe, 32), :] = zero

    for t in range(3):
        wb[t, z, pl.ds(off, BLK), :] = own[t][...]

    advance((0, 1), 2)
    advance((0, 1), 3)
    advance((2, 3), 0)
    advance((0, 1), 4)
    own_tokens.wait()
    for copy in tokens:
        copy.wait_recv()

    def multiply(t):
        acc[t] = jnp.zeros(acc.shape[1:], F32)

        @pl.loop(0, Z)
        def _(c):
            acc[t] += jnp.dot(xg[c], wb[t, c], preferred_element_type=F32)

        copies = []
        for d in range(1, X):
            there = lax.rem(x + d, X)
            part[t, d - 1] = acc[t, pl.ds(pl.multiple_of(there * 128, 128), 128), :].astype(BF16)
            copy = remote(
                part.at[t, d - 1], got.at[t, d - 1], part_send.at[t, d - 1], part_recv.at[t, d - 1], at(0, d)
            )
            copy.start()
            copies.append(copy)
        return copies

    def collect(t, copies):
        total = acc[t, mine, :]
        for copy in copies:
            copy.wait_recv()
        for d in range(1, X):
            total = total + got[t, d - 1].astype(F32)
        return total

    def turn(rows):
        pieces = []
        for h in range(rows.shape[1] // HD):
            piece = rows[:, h * HD : (h + 1) * HD]
            pieces.append(piece * cos_ref[...] + pltpu.roll(piece, HD // 2, 1) * sin_ref[...])
        return jnp.concatenate(pieces, axis=1).astype(BF16)

    q_copies = multiply(0)
    k_copies = multiply(1)
    advance((2, 3), 1)
    query = turn(collect(0, q_copies))
    for r in range(qloc.shape[0]):
        qloc[r] = query[r * 16 : (r + 1) * 16]
    own_query = pltpu.make_async_copy(qloc, q_all.at[:, seq], local_sem.at[2])
    own_query.start()

    def to_z(d):
        return remote(qloc, q_all.at[:, seq], zq_send.at[d - 1], zq_recv.at[d - 1], at(d, 0))

    def to_x(dz, d):
        slot = q_all.at[:, lax.rem(z - dz + Z, Z) * X + x]
        return remote(qloc if dz == 0 else slot, slot, xq_send.at[d - 1, dz], xq_recv.at[d - 1, dz], at(0, d))

    arrival = sorted(range(1, Z), key=lambda d: min(d, Z - d))
    for d in arrival:
        to_z(d).start()
    for d in range(1, X):
        to_x(0, d).start()
    advance((2, 3), 2)
    kn_ref[...] = turn(collect(1, k_copies))
    advance((2, 3), 3)
    for d in arrival[: Z // 2]:
        to_z(d).wait_recv()
        for e in range(1, X):
            to_x(d, e).start()
    advance((2, 3), 4)
    v_copies = multiply(2)
    for d in arrival[Z // 2 :]:
        to_z(d).wait_recv()
        for e in range(1, X):
            to_x(d, e).start()
    vn_ref[...] = collect(2, v_copies).astype(BF16)

    own_out.wait()
    own_query.wait()
    for t in range(4):
        for right in (True, False):
            for k in range(steps(t, right)):
                ring(right, t, k).wait_send()
    for copy in tokens + q_copies + k_copies + v_copies:
        copy.wait_send()
    for d in range(1, Z):
        to_z(d).wait_send()
    for dz in range(Z):
        for d in range(1, X):
            to_x(dz, d).wait()


def project(Z, block_input, accepted, mask, gain, cosine, sine, w_query, w_key, w_value, w_out):
    requests = block_input.shape[0]
    cols = w_query.shape[1]
    rows = requests * 16
    vmem = pl.BlockSpec(memory_space=pltpu.VMEM)
    hbm = pl.BlockSpec(memory_space=pl.ANY)
    dma = pltpu.SemaphoreType.DMA
    return pl.pallas_call(
        functools.partial(project_kernel, Z),
        name="project",
        out_shape=(
            jax.ShapeDtypeStruct((requests, Z * X, 16, cols), BF16),
            jax.ShapeDtypeStruct((rows, cols), BF16),
            jax.ShapeDtypeStruct((rows, cols), BF16),
            jax.ShapeDtypeStruct((Z, BLK, cols), BF16),
        ),
        in_specs=[vmem] * 10,
        out_specs=(hbm, vmem, vmem, hbm),
        scratch_shapes=[
            pltpu.VMEM((Z, rows, X * BLK), BF16),
            pltpu.VMEM((Z, X * rows, COVER), BF16),
            pltpu.VMEM((3, Z, COVER, cols), BF16),
            pltpu.VMEM((3, X * rows, cols), F32),
            pltpu.VMEM((3, X - 1, rows, cols), BF16),
            pltpu.VMEM((3, X - 1, rows, cols), BF16),
            pltpu.VMEM((requests, 16, cols), BF16),
            dma((2, 4, Z // 2)),
            dma((2, 4, Z // 2)),
            dma((X - 1,)),
            dma((X - 1,)),
            dma((3, X - 1)),
            dma((3, X - 1)),
            dma((Z - 1,)),
            dma((Z - 1,)),
            dma((X - 1, Z)),
            dma((X - 1, Z)),
            dma((3,)),
        ],
        compiler_params=pltpu.CompilerParams(
            collective_id=0, has_side_effects=True, vmem_limit_bytes=44 << 20
        ),
    )(block_input, accepted, mask, gain, cosine, sine, w_query, w_key, w_value, w_out)


def attend_kernel(owner, live, q_ref, k_ref, v_ref, kn_ref, vn_ref, o_ref, st_ref, acc, stats):
    r = pl.program_id(0)
    heads = acc.shape[0]
    queries = acc.shape[2]
    scale = HD ** (-0.5)

    @pl.when(r == 0)
    def _():
        stats[...] = jnp.zeros_like(stats)

    key_pass = lax.broadcasted_iota(jnp.int32, (16, queries), 0) // 8
    query_pass = lax.rem(lax.broadcasted_iota(jnp.int32, (16, queries), 1) // 8, 2)
    same = key_pass == query_pass
    for h in range(heads):
        col = slice(h * HD, (h + 1) * HD)
        scores = lax.dot_general(kn_ref[0, :, col], q_ref[0, :, col], NT, preferred_element_type=F32) * scale
        scores = jnp.where(same, scores, -1e30)
        peak = jnp.max(scores, axis=0, keepdims=True)
        weights = jnp.where(same, jnp.exp(scores - peak), 0.0)
        high = weights.astype(BF16)
        low = (weights - high.astype(F32)).astype(BF16)
        values = vn_ref[0, :, col]
        acc[h] = lax.dot_general(
            jnp.concatenate([values, values], axis=0),
            jnp.concatenate([high, low], axis=0),
            TN,
            preferred_element_type=F32,
        )
        stats[pl.ds(r * 8 + h, 1), :] = peak
        stats[pl.ds(r * 8 + 4 + h, 1), :] = jnp.sum(weights, axis=0, keepdims=True)

    slot = lax.broadcasted_iota(jnp.int32, (PAGE, queries), 0)

    @pl.loop(0, k_ref.shape[0])
    def _(p):
        @pl.when(jnp.logical_and(owner[p] == r, live[p] > 0))
        def _():
            alive = slot < live[p]
            for h in range(heads):
                col = slice(h * HD, (h + 1) * HD)
                scores = lax.dot_general(k_ref[p, :, col], q_ref[0, :, col], NT, preferred_element_type=F32) * scale
                scores = jnp.where(alive, scores, -1e30)
                page_peak = jnp.max(scores, axis=0, keepdims=True)
                weights = jnp.where(alive, jnp.exp(scores - page_peak), 0.0)
                page_out = lax.dot_general(
                    v_ref[p, :, col], weights.astype(BF16), TN, preferred_element_type=F32
                )
                m_row = pl.ds(r * 8 + h, 1)
                l_row = pl.ds(r * 8 + 4 + h, 1)
                before = stats[m_row, :]
                after = jnp.maximum(before, page_peak)
                old, new = jnp.exp(before - after), jnp.exp(page_peak - after)
                acc[h] = acc[h] * old + page_out * new
                stats[m_row, :] = after
                stats[l_row, :] = stats[l_row, :] * old + jnp.sum(weights, axis=0, keepdims=True) * new

    for h in range(heads):
        o_ref[0, :, h * HD : (h + 1) * HD] = jnp.transpose(acc[h]).astype(BF16)

    @pl.when(r == pl.num_programs(0) - 1)
    def _():
        st_ref[...] = jnp.transpose(stats[...])


def attend(owner, live, q_all, key_cache, value_cache, new_keys, new_values):
    requests, queries, cols = q_all.shape
    pages = key_cache.shape[0]
    heads = cols // HD
    return pl.pallas_call(
        attend_kernel,
        name="attend",
        out_shape=(
            jax.ShapeDtypeStruct((requests, queries, cols), BF16),
            jax.ShapeDtypeStruct((queries, 128), F32),
        ),
        grid_spec=pltpu.PrefetchScalarGridSpec(
            num_scalar_prefetch=2,
            grid=(requests,),
            in_specs=[
                pl.BlockSpec((1, queries, cols), lambda r, *_: (r, 0, 0)),
                pl.BlockSpec((pages, PAGE, cols), lambda r, *_: (0, 0, 0)),
                pl.BlockSpec((pages, PAGE, cols), lambda r, *_: (0, 0, 0)),
                pl.BlockSpec((1, 16, cols), lambda r, *_: (r, 0, 0)),
                pl.BlockSpec((1, 16, cols), lambda r, *_: (r, 0, 0)),
            ],
            out_specs=[
                pl.BlockSpec((1, queries, cols), lambda r, *_: (r, 0, 0)),
                pl.BlockSpec((queries, 128), lambda r, *_: (0, 0)),
            ],
            scratch_shapes=[
                pltpu.VMEM((heads, HD, queries), F32),
                pltpu.VMEM((128, queries), F32),
            ],
        ),
        compiler_params=pltpu.CompilerParams(vmem_limit_bytes=40 << 20),
    )(owner, live, q_all, key_cache, value_cache, new_keys, new_values)


def join(tables, pieces, emit):
    peak = functools.reduce(jnp.maximum, tables)
    factors = [jnp.exp(table - peak) for table in tables]
    shifted = [pltpu.roll(factor, 4, 1) for factor in factors]
    total = sum(s * table for s, table in zip(shifted, tables))
    lane = lax.broadcasted_iota(jnp.int32, peak.shape, 1)
    table = jnp.where(lax.rem(lane, 8) >= 4, total, peak)
    emit(table, factors)


def finish_kernel(
    Z,
    o_ref,
    st_ref,
    wo_ref,
    first_ref,
    second_ref,
    oown,
    ra,
    ra_st,
    cb,
    cb_st,
    rb,
    rb_st,
    ctx,
    pb,
    ph,
    ob,
    of,
    a_send,
    a_recv,
    as_send,
    as_recv,
    b_send,
    b_recv,
    bs_send,
    bs_recv,
    c_send,
    c_recv,
    d_send,
    d_recv,
    e_send,
    e_recv,
    local_sem,
):
    seq, head, z, x, at = place(Z)
    requests = oown.shape[0]
    heads = oown.shape[3] // HD

    def other(d):
        return (seq, lax.rem(head + d, Z))

    greet(
        [at(d, 0) for d in range(1, Z)]
        + [at(0, d) for d in range(1, X)]
        + [other(d) for d in range(1, Z)]
    )

    def to_x(zi, d):
        there = lax.rem(z + zi, Z)
        return remote(
            o_ref.at[:, there, lax.rem(x + d, X)],
            ra.at[d - 1, there],
            a_send.at[d - 1, zi],
            a_recv.at[d - 1, zi],
            at(0, d),
        )

    def to_x_st(d):
        return remote(
            st_ref.at[:, lax.rem(x + d, X)], ra_st.at[d - 1], as_send.at[d - 1], as_recv.at[d - 1], at(0, d)
        )

    own = pltpu.make_async_copy(o_ref.at[:, :, x], oown, local_sem.at[0])
    own.start()
    for d in range(1, X):
        to_x_st(d).start()

    @pl.loop(1, Z + 1)
    def _(i):
        zi = lax.rem(i, Z)
        for d in range(1, X):
            to_x(zi, d).start()

    own.wait()
    for d in range(1, X):
        to_x_st(d).wait_recv()

    def to_z(zi):
        there = lax.rem(z + zi, Z)
        target = (there * X + x, head)
        return (
            remote(cb.at[there], rb.at[zi - 1], b_send.at[zi - 1], b_recv.at[zi - 1], target),
            remote(cb_st.at[there], rb_st.at[zi - 1], bs_send.at[zi - 1], bs_recv.at[zi - 1], target),
        )

    def gather_x(zi):
        there = lax.rem(z + zi, Z)
        for d in range(1, X):
            to_x(zi, d).wait_recv()
        tables = [st_ref[there, x]] + [ra_st[d - 1, there] for d in range(1, X)]

        def emit(table, factors):
            cb_st[there] = table
            for r in range(requests):
                sources = [oown[r, there]] + [ra[d - 1, there, r] for d in range(1, X)]
                for h in range(heads):
                    col = slice(h * HD, (h + 1) * HD)
                    lane = r * 8 + h
                    value = sum(
                        factor[:, lane : lane + 1] * source[:, col].astype(F32)
                        for factor, source in zip(factors, sources)
                    )
                    cb[there, r, :, col] = value.astype(BF16)

        join(tables, None, emit)

    @pl.loop(1, Z)
    def _(zi):
        gather_x(zi)
        for copy in to_z(zi):
            copy.start()

    gather_x(0)
    for d in range(1, Z):
        for copy in to_z(d):
            copy.wait_recv()

    mine = pl.multiple_of(x * 128, 128)

    def emit(table, factors):
        inverse = 1.0 / table
        for r in range(requests):
            sources = [cb[z, r]] + [rb[d - 1, r] for d in range(1, Z)]
            for h in range(heads):
                col = slice(h * HD, (h + 1) * HD)
                lane = r * 8 + h
                value = sum(
                    factor[:, lane : lane + 1] * source[:, col].astype(F32)
                    for factor, source in zip(factors, sources)
                )
                value = value * inverse[:, lane + 4 : lane + 5]
                ctx[pl.ds(mine + r * 16, 16), col] = value.astype(BF16)

    join([cb_st[z]] + [rb_st[d - 1] for d in range(1, Z)], None, emit)

    rows = pl.ds(mine, 128)
    shares = [remote(ctx.at[rows], ctx.at[rows], c_send.at[d - 1], c_recv.at[d - 1], at(0, d)) for d in range(1, X)]
    for copy in shares:
        copy.start()
    for copy in shares:
        copy.wait_recv()

    def to_head(d):
        return remote(pb.at[d - 1], ph.at[d - 1], d_send.at[d - 1], d_recv.at[d - 1], other(d))

    def partial(d):
        return lax.dot_general(wo_ref[lax.rem(head + d, Z)], ctx[...], NT, preferred_element_type=F32)

    @pl.loop(1, Z)
    def _(d):
        pb[d - 1] = partial(d).astype(BF16)
        to_head(d).start()

    total = partial(0)
    for d in range(1, Z):
        to_head(d).wait_recv()
        total = total + ph[d - 1].astype(F32)
    ob[...] = total.astype(BF16)
    block = pl.ds(pl.multiple_of(x * BLK, 32), BLK)

    def to_owner(d):
        there = pl.multiple_of(lax.rem(x + d, X) * 128, 128)
        return remote(ob.at[:, pl.ds(there, 128)], of.at[block], e_send.at[d - 1], e_recv.at[d - 1], at(0, d))

    for d in range(1, X):
        to_owner(d).start()
    last = pltpu.make_async_copy(ob.at[:, pl.ds(mine, 128)], of.at[block], local_sem.at[1])
    last.start()
    last.wait()
    for d in range(1, X):
        to_owner(d).wait_recv()
    result = jnp.transpose(of[...].astype(F32))
    for r in range(requests):
        first_ref[r] = result[r * 16 : r * 16 + 8].astype(BF16)
        second_ref[r] = result[r * 16 + 8 : r * 16 + 16].astype(BF16)

    for d in range(1, X):
        to_x_st(d).wait_send()
        shares[d - 1].wait_send()
        to_owner(d).wait_send()

        @pl.loop(0, Z)
        def _(zi):
            to_x(zi, d).wait_send()

    for d in range(1, Z):
        for copy in to_z(d):
            copy.wait_send()
        to_head(d).wait_send()


def finish(Z, out, table, wo_all, tokens):
    requests = out.shape[0]
    cols = out.shape[4]
    rows = requests * 16
    vmem = pl.BlockSpec(memory_space=pltpu.VMEM)
    hbm = pl.BlockSpec(memory_space=pl.ANY)
    dma = pltpu.SemaphoreType.DMA
    shape = jax.ShapeDtypeStruct((requests, tokens, X * BLK), BF16)
    return pl.pallas_call(
        functools.partial(finish_kernel, Z),
        name="finish",
        out_shape=(shape, shape),
        in_specs=[hbm, vmem, vmem],
        out_specs=(vmem, vmem),
        scratch_shapes=[
            pltpu.VMEM((requests, Z, 16, cols), BF16),
            pltpu.VMEM((X - 1, Z, requests, 16, cols), BF16),
            pltpu.VMEM((X - 1, Z, 16, 128), F32),
            pltpu.VMEM((Z, requests, 16, cols), BF16),
            pltpu.VMEM((Z, 16, 128), F32),
            pltpu.VMEM((Z - 1, requests, 16, cols), BF16),
            pltpu.VMEM((Z - 1, 16, 128), F32),
            pltpu.VMEM((X * rows, cols), BF16),
            pltpu.VMEM((Z - 1, BLK, X * rows), BF16),
            pltpu.VMEM((Z - 1, BLK, X * rows), BF16),
            pltpu.VMEM((BLK, X * rows), BF16),
            pltpu.VMEM((X * BLK, rows), BF16),
            dma((X - 1, Z)),
            dma((X - 1, Z)),
            dma((X - 1,)),
            dma((X - 1,)),
            dma((Z - 1,)),
            dma((Z - 1,)),
            dma((Z - 1,)),
            dma((Z - 1,)),
            dma((X - 1,)),
            dma((X - 1,)),
            dma((Z - 1,)),
            dma((Z - 1,)),
            dma((X - 1,)),
            dma((X - 1,)),
            dma((2,)),
        ],
        compiler_params=pltpu.CompilerParams(
            collective_id=1, has_side_effects=True, vmem_limit_bytes=44 << 20
        ),
    )(out, table, wo_all)


def per_device(
    Z,
    block_input,
    accepted,
    accept_mask,
    cache_lengths,
    page_table,
    norm_gain,
    w_query,
    w_key,
    w_value,
    w_out,
    key_cache,
    value_cache,
):
    seq = lax.axis_index("seq")
    requests, tokens, width = block_input.shape
    half = HD // 2
    frequency = 10000.0 ** (-(jnp.arange(half).astype(F32) * 2.0) / HD)
    positions = (
        cache_lengths[:, None] + seq * tokens + jnp.arange(tokens, dtype=jnp.int32)[None, :]
    ).astype(F32)
    angles = jnp.broadcast_to(positions[:, None, :, None] * frequency, (requests, 2, tokens, half))
    angles = angles.reshape(requests * 2 * tokens, half)
    cosine, sine = jnp.cos(angles), jnp.sin(angles)
    cosine = jnp.concatenate([cosine, cosine], axis=1)
    sine = jnp.concatenate([-sine, sine], axis=1)

    pages_here = key_cache.shape[0]
    page_ids = seq * pages_here + jnp.arange(pages_here, dtype=jnp.int32)
    table_slots = jnp.arange(page_table.shape[0], dtype=jnp.int32)
    slot_of = jnp.sum(
        jnp.where(page_table[None, :] == page_ids[:, None], table_slots[None, :], 0), axis=1
    )
    owner = slot_of // MAXP
    owner_match = owner[:, None] == jnp.arange(requests, dtype=jnp.int32)[None, :]
    owner_length = jnp.sum(jnp.where(owner_match, cache_lengths[None, :], 0), axis=1)
    live = owner_length - (slot_of % MAXP) * PAGE

    q_all, new_keys, new_values, wo_all = project(
        Z,
        block_input,
        accepted,
        accept_mask.reshape(requests, tokens, 1),
        norm_gain.reshape(1, width),
        cosine,
        sine,
        w_query,
        w_key,
        w_value,
        w_out,
    )
    cols = q_all.shape[3]
    queries = Z * X * 16
    out, table = attend(
        owner,
        live,
        q_all.reshape(requests, queries, cols),
        key_cache,
        value_cache,
        new_keys.reshape(requests, 16, cols),
        new_values.reshape(requests, 16, cols),
    )
    return finish(
        Z,
        out.reshape(requests, Z, X, 16, cols),
        table.reshape(Z, X, 16, 128),
        wo_all,
        tokens,
    )


def solution(mesh):
    placed = (
        P(None, "seq", None),
        P(None, "seq", None),
        P(None, "seq"),
        P(),
        P(),
        P(),
        P("seq", "head"),
        P("seq", "head"),
        P("seq", "head"),
        P("seq", "head"),
        P("seq", None, "head"),
        P("seq", None, "head"),
    )
    return jax.shard_map(
        functools.partial(per_device, mesh.shape["seq"] // X),
        mesh=mesh,
        in_specs=placed,
        out_specs=(P(None, "seq", "head"), P(None, "seq", "head")),
        check_vma=False,
    )
```

time: 920 us -> 212 us (0.23)
  waiting for transfers between devices: 540 us -> 0 us
  blocking collectives: 221 us -> 0 us
  Pallas kernels: 0 us -> 198 us
  matrix products: 64.6 us -> 0 us
  local copies, waits for them, and re-layouts: 53.1 us -> 10 us
  other arithmetic: 21.4 us -> 2.79 us
  between operations: 14.9 us -> 0.74 us
    all_gather x5 -> x0, waiting for transfers between devices: 363 us -> none  [the longest x1 82.5 us: per_device(): lax.all_gather(w_out, 'seq', axis=0, tiled=True)]
    pallas_call x0 -> x3, Pallas kernels: none -> 198 us  [the longest x1 99.3 us: project(): pl.pallas_call(functools.partial(project_kernel, Z), name='project', out_...]
    reduce_scatter x2 -> x0, waiting for transfers between devices: 175 us -> none  [the longest x1 140 us: per_device(): lax.psum_scatter(row_out * rescale[..., None], 'seq', scatter_dimension=2...]
    unnamed x1 -> x0, blocking collectives: 112 us -> none
    pmax x1 -> x0, blocking collectives: 109 us -> none  [per_device(): overall = lax.pmax(row_peak, 'seq')]
    dot_general x16 -> x0, matrix products: 64.6 us -> none  [the longest x2 22.4 us: local_part(): jnp.einsum('pr,pqhd->rqhd', owner_hot, page_out * factor[..., None], prec...]
    dot_general x5 -> x0, local copies, waits for them, and re-layouts: 23.5 us -> none  [the longest x1 6.33 us: per_device(): jnp.dot(token_rows, full_query, preferred_element_type=jnp.float32)]
  transfers between devices with their start and end apart: 7 -> 0, of which waited for: 7 -> 0; matrix products, arithmetic and copies ran while one was open for 5% -> 0% of each run, Pallas kernels for 0% -> 0%
where the time goes in v1:
time: 212 us; the launch traced here: 211 us
  Pallas kernels  198 us (93%)
  local copies, waits for them, and re-layouts  10 us (5%)
  other arithmetic  2.79 us (1%)
    pallas_call x1, Pallas kernels, project(): pl.pallas_call(functools.partial(project_kernel, Z), name='project', out_...  99.3 us
    pallas_call x1, Pallas kernels, finish(): pl.pallas_call(functools.partial(finish_kernel, Z), name='finish', out_sh...  80.9 us
    pallas_call x1, Pallas kernels, attend(): pl.pallas_call(attend_kernel, name='attend', out_shape=(jax.ShapeDtypeStr...  17.5 us
    unnamed x20, local copies, waits for them, and re-layouts  9.18 us

profile of v1, /device:TPU:33, one launch (start us, length us, event | category | flops | bytes accessed | tf_op | source)
XLA Modules:
  0.0 211.2 jit_solution(14122056104855824173)
XLA Ops:
  0.6 0.0 copy-start
  0.6 0.8 broadcast_add_fusion
  1.4 0.9 select_reduce_fusion
  2.3 0.7 select_reduce_fusion.1
  3.1 0.1 add_convert_fusion
  3.1 0.8 copy.15.mask_ref
  3.9 0.2 multiply_sine_fusion
  4.2 0.1 pad_maximum_fusion
  4.3 0.0 copy-start.2
  4.3 1.1 copy-done.2
  5.4 0.0 copy-start.3
  5.4 1.1 copy-done.3
  6.5 0.0 copy-start.4
  6.5 0.9 copy-done.4
  7.4 0.0 copy-start.5
  7.4 0.9 copy-done.5
  8.3 0.0 copy-start.6
  8.3 0.9 copy-done.6
  9.2 0.0 copy-start.7
  9.2 0.9 copy-done.7
  10.1 0.0 copy-start.8
  10.1 0.7 copy-done.8
  10.8 99.3 %project.1 = (bf16[8,32,16,384]{3,2,1,0:T(8,128)(2,1)S(1)}, bf16[128,384]{1,0:T(8,128)(2,1)S(1)}, bf16[128,384]{1,0:T(8,128)(2,1)S(1)}, bf16[8,160,384]{2,1,0:T(8,128)(2,1)S(1)}) custom-call(bf16[8,8,5120]{2,1,0:T(8,128)(2,1)S(1)} %copy-done.2, bf16[8,8,5120]{2,1,0:T(8,128)(2,1)S(1)} %copy-done.3, s32[8,8,1]{2,1,0:T(8,128)S(1)} %copy.15.mask_ref, ...), custom_call_target="tpu_custom_call" | custom-call | tf_op jit(solution)/shard_map/project/pallas_call | solution.py:252
  110.2 0.0 copy-done
  110.2 0.0 copy-start.1
  110.2 1.4 copy-done.1
  111.6 17.5 %attend.1 = (bf16[8,512,384]{2,1,0:T(8,128)(2,1)S(1)}, f32[512,128]{1,0:T(8,128)S(1)}) custom-call(s32[16]{0:T(128)S(1)} %and_select_fusion.1.owner, s32[16]{0:T(128)S(1)} %fusion.1.live, bf16[8,512,384]{2,1,0:T(8,128)(2,1)S(1)} %bitcast.11, bf16[16,128,384]{2,1,0:T(8,128)(2,1)S(1)} %copy-done, bf16[16,128,384]{2,1,0:T(8,128)(2,1)S(1)} %copy-done.1, ...), custom_call_target="tpu_custom_call" | custom-call | tf_op jit(solution)/shard_map/attend/pallas_call | solution.py:357
  129.0 80.9 %finish.1 = (bf16[8,8,640]{2,1,0:T(8,128)(2,1)S(1)}, bf16[8,8,640]{2,1,0:T(8,128)(2,1)S(1)}) custom-call(bf16[8,8,4,16,384]{4,3,2,1,0:T(8,128)(2,1)S(1)} %bitcast.10, f32[8,4,16,128]{3,2,1,0:T(8,128)S(1)} %bitcast.12, bf16[8,160,384]{2,1,0:T(8,128)(2,1)S(1)} %get-tuple-element.13.wo_ref), custom_call_target="tpu_custom_call" | custom-call | tf_op jit(solution)/shard_map/finish/pallas_call | solution.py:597
  209.9 0.6 copy.18
  210.5 0.6 copy.19
  (7 shorter events, 0.1 us)
Async XLA Ops:
  0.6 109.5 %copy-start = (bf16[16,128,384]{2,1,0:T(8,128)(2,1)S(1)}, bf16[16,128,384]{2,1,0:T(8,128)(2,1)}, u32[]{:S(2)}) copy-start(bf16[16,128,384]{2,1,0:T(8,128)(2,1)} %k_ref.1) | copy-start | bytes 4718596
  4.3 1.1 copy-start.2
  5.4 1.1 copy-start.3
  6.5 0.9 copy-start.4
  7.4 0.9 copy-start.5
  8.3 0.9 copy-start.6
  9.2 0.9 copy-start.7
  10.1 0.7 copy-start.8
  110.2 1.4 copy-start.1

commit v2 on v1

v2 whole, which is shorter than its diff:
```python
import functools

import jax
import jax.numpy as jnp
from jax import lax
from jax.experimental import pallas as pl
from jax.experimental.pallas import tpu as pltpu
from jax.sharding import PartitionSpec as P

HD = 128
PAGE = 128
MAXP = 64
X = 4
BLK = 160
COVER = 256
MESH = pl.DeviceIdType.MESH
F32 = jnp.float32
BF16 = jnp.bfloat16
NT = (((1,), (1,)), ((), ()))
TN = (((0,), (0,)), ((), ()))


def in_hbm(*arrays):
    return [pltpu.with_memory_space_constraint(array, pltpu.HBM) for array in arrays]


def place(Z):
    seq = lax.axis_index("seq")
    head = lax.axis_index("head")
    z, x = seq // X, lax.rem(seq, X)

    def at(dz, dx):
        return (lax.rem(z + dz + Z, Z) * X + lax.rem(x + dx, X), head)

    return seq, head, z, x, at


def greet(partners):
    barrier = pltpu.get_barrier_semaphore()
    for partner in partners:
        pl.semaphore_signal(barrier, inc=1, device_id=partner, device_id_type=MESH)
    pl.semaphore_wait(barrier, len(partners))


def remote(src, dst, send, recv, target):
    return pltpu.make_async_remote_copy(
        src_ref=src, dst_ref=dst, send_sem=send, recv_sem=recv, device_id=target, device_id_type=MESH
    )


def project_kernel(
    Z,
    x_hbm,
    a_hbm,
    mask_hbm,
    gain_hbm,
    cos_ref,
    sin_ref,
    wq_ref,
    wk_ref,
    wv_ref,
    q_all,
    kn_ref,
    vn_ref,
    xs,
    as_,
    mask_ref,
    gain,
    xn,
    xg,
    wb,
    acc,
    part,
    got,
    qloc,
    ring_send,
    ring_recv,
    tok_send,
    tok_recv,
    core_send,
    core_recv,
    part_send,
    part_recv,
    zq_send,
    zq_recv,
    xq_send,
    xq_recv,
    local_sem,
):
    seq, head, z, x, at = place(Z)
    width = X * BLK
    off = pl.multiple_of(32 * x, 32)
    own = (wq_ref, wk_ref, wv_ref)
    half = xs.shape[0]
    core = lax.rem(head, 2)
    partner = (seq, head + 1 - 2 * core)
    ours = pl.ds(core * half, half)
    loads = [
        pltpu.make_async_copy(x_hbm.at[ours], xs, local_sem.at[0]),
        pltpu.make_async_copy(a_hbm.at[ours], as_, local_sem.at[1]),
        pltpu.make_async_copy(gain_hbm, gain, local_sem.at[2]),
        pltpu.make_async_copy(mask_hbm, mask_ref, local_sem.at[8]),
    ]
    for copy in loads:
        copy.start()
    kept = [pltpu.make_async_copy(own[t], wb.at[t, z, pl.ds(off, BLK)], local_sem.at[3 + t]) for t in range(3)]
    for copy in kept:
        copy.start()
    greet([at(d, 0) for d in range(1, Z)] + [at(0, d) for d in range(1, X)] + [partner])

    def ring(right, t, k):
        block = lax.rem(z - k + Z, Z) if right else lax.rem(z + k, Z)
        slot = wb.at[t, block, pl.ds(off, BLK)]
        src = own[t] if k == 0 else slot
        way = 1 if right else 0
        return remote(
            src, slot, ring_send.at[way, t, k], ring_recv.at[way, t, k], at(1 if right else -1, 0)
        )

    def steps(t, right):
        return Z // 2 if right == (t % 2 == 0) else Z - 1 - Z // 2

    def advance(tensors, k):
        for t in tensors:
            for right in (True, False):
                if 0 < k <= steps(t, right):
                    ring(right, t, k - 1).wait_recv()
                if k < steps(t, right):
                    ring(right, t, k).start()

    advance((0, 1), 0)
    for copy in loads:
        copy.wait()

    diagonal = lax.broadcasted_iota(jnp.int32, (8, 8), 0) == lax.broadcasted_iota(jnp.int32, (8, 8), 1)

    @pl.loop(0, half)
    def _(r):
        accept = mask_ref[pl.ds(core * half + r, 1), :].astype(F32)
        accept = jnp.sum(jnp.where(diagonal, accept, 0.0), axis=1, keepdims=True)
        first = xs[r].astype(F32)
        second = jnp.where(accept == 1.0, as_[r].astype(F32), first)
        both = jnp.concatenate([first, second], axis=0)
        inverse = lax.rsqrt(jnp.mean(both * both, axis=-1, keepdims=True) + 1e-05)
        normed = (both * inverse * gain[...]).astype(BF16)
        rows = pl.ds(pl.multiple_of(r * 16, 16), 16)
        for c in range(Z):
            xn[c, rows, :] = normed[:, c * width : (c + 1) * width]

    share = half * 16
    mine = pl.ds(pl.multiple_of(x * 128, 128), 128)

    def cover(there):
        return xn.at[:, :, pl.ds(pl.multiple_of(there * 128, 128), COVER)]

    def rows_of(source):
        return xg.at[:, pl.ds(pl.multiple_of(source * 128 + core * share, share), share)]

    def token(d):
        return remote(cover(lax.rem(x + d, X)), rows_of(x), tok_send.at[d - 1], tok_recv.at[d - 1], at(0, d))

    def across(d):
        slot = rows_of(lax.rem(x - d + X, X))
        return remote(cover(x) if d == 0 else slot, slot, core_send.at[d], core_recv.at[d], partner)

    for d in (2, 1, 3):
        token(d).start()
    across(0).start()
    own_tokens = pltpu.make_async_copy(cover(x), rows_of(x), local_sem.at[6])
    own_tokens.start()

    zero = jnp.zeros((32, wb.shape[3]), BF16)

    @pl.loop(0, Z)
    def _(c):
        for t in range(3):
            for j in range(3):
                stripe = pl.multiple_of(32 * lax.rem(x + 5 + j, 8), 32)
                wb[t, c, pl.ds(stripe, 32), :] = zero

    acc[...] = jnp.zeros_like(acc)
    advance((0, 1), 1)
    advance((0, 1), 2)
    for d in (1, 3, 2):
        token(d).wait_recv()
        across(d).start()
    advance((0, 1), 3)
    advance((2,), 0)
    own_tokens.wait()
    for copy in kept:
        copy.wait()
    for d in range(X):
        across(d).wait_recv()

    def multiply(t, low, high):
        @pl.loop(low, high)
        def _(j):
            block = lax.rem(z + (1 - 2 * lax.rem(j, 2)) * ((j + 1) // 2) + Z, Z)
            acc[t] += jnp.dot(xg[block], wb[t, block], preferred_element_type=F32)

    def piece(t, d):
        return remote(
            part.at[t, d - 1], got.at[t, d - 1], part_send.at[t, d - 1], part_recv.at[t, d - 1], at(0, d)
        )

    def spread(t):
        for d in (2, 1, 3):
            there = lax.rem(x + d, X)
            part[t, d - 1] = acc[t, pl.ds(pl.multiple_of(there * 128, 128), 128), :].astype(BF16)
            piece(t, d).start()

    def collect(t):
        total = acc[t, mine, :]
        for d in range(1, X):
            piece(t, d).wait_recv()
            total = total + got[t, d - 1].astype(F32)
        return total

    def turn(rows):
        pieces = []
        for h in range(rows.shape[1] // HD):
            piece = rows[:, h * HD : (h + 1) * HD]
            pieces.append(piece * cos_ref[...] + pltpu.roll(piece, HD // 2, 1) * sin_ref[...])
        return jnp.concatenate(pieces, axis=1).astype(BF16)

    multiply(0, 0, Z - 1)
    multiply(1, 0, Z - 1)
    advance((0, 1), 4)
    multiply(0, Z - 1, Z)
    spread(0)
    multiply(1, Z - 1, Z)
    spread(1)
    advance((2,), 1)
    query = turn(collect(0))
    for r in range(qloc.shape[0]):
        qloc[r] = query[r * 16 : (r + 1) * 16]
    own_query = pltpu.make_async_copy(qloc, q_all.at[:, seq], local_sem.at[7])
    own_query.start()

    def to_z(right, k):
        slot = q_all.at[:, (lax.rem(z - k + Z, Z) if right else lax.rem(z + k, Z)) * X + x]
        i = 1 if right else 0
        return remote(
            qloc if k == 0 else slot, slot, zq_send.at[i, k], zq_recv.at[i, k], at(1 if right else -1, 0)
        )

    hops = {True: Z // 2, False: Z - 1 - Z // 2}

    def to_x(dz, way):
        slot = q_all.at[:, lax.rem(z - dz + Z, Z) * X + x]
        i = (way + 1) // 2
        return remote(qloc if dz == 0 else slot, slot, xq_send.at[i, 0, dz], xq_recv.at[i, 0, dz], at(0, way + X))

    def onward(dz):
        way = 1 - 2 * (dz % 2)
        slot = q_all.at[:, lax.rem(z - dz + Z, Z) * X + lax.rem(x - way + X, X)]
        i = (way + 1) // 2
        return remote(slot, slot, xq_send.at[i, 1, dz], xq_recv.at[i, 1, dz], at(0, way + X))

    arrival = [0] + sorted(range(1, Z), key=lambda d: min(d, Z - d))

    def pass_on(low, high):
        for i in range(low, high):
            if i < Z:
                dz = arrival[i]
                if dz:
                    right = dz <= hops[True]
                    k = dz if right else Z - dz
                    to_z(right, k - 1).wait_recv()
                    if k < hops[right]:
                        to_z(right, k).start()
                to_x(dz, 1).start()
                to_x(dz, -1).start()
            if i > 0:
                dz = arrival[i - 1]
                to_x(dz, 1 - 2 * (dz % 2)).wait_recv()
                onward(dz).start()

    to_z(True, 0).start()
    to_z(False, 0).start()
    pass_on(0, 1)
    advance((2,), 2)
    kn_ref[...] = turn(collect(1))
    advance((2,), 3)
    pass_on(1, 3)
    advance((2,), 4)
    multiply(2, 0, Z)
    spread(2)
    pass_on(3, Z + 1)
    vn_ref[...] = collect(2).astype(BF16)

    own_query.wait()
    for t in range(3):
        for right in (True, False):
            for k in range(steps(t, right)):
                ring(right, t, k).wait_send()
        for d in range(1, X):
            piece(t, d).wait_send()
    for d in range(1, X):
        token(d).wait_send()
    for d in range(X):
        across(d).wait_send()
    for right in (True, False):
        for k in range(hops[right]):
            to_z(right, k).wait_send()
    for dz in range(Z):
        forwarded = 1 - 2 * (dz % 2)
        to_x(dz, -forwarded).wait_recv()
        onward(dz).wait()
        to_x(dz, 1).wait_send()
        to_x(dz, -1).wait_send()


def project(Z, block_input, accepted, mask, gain, cosine, sine, w_query, w_key, w_value):
    requests, tokens, width = block_input.shape
    cols = w_query.shape[1]
    rows = requests * 16
    vmem = pl.BlockSpec(memory_space=pltpu.VMEM)
    hbm = pl.BlockSpec(memory_space=pltpu.HBM)
    dma = pltpu.SemaphoreType.DMA
    return pl.pallas_call(
        functools.partial(project_kernel, Z),
        name="project",
        out_shape=(
            jax.ShapeDtypeStruct((requests, Z * X, 16, cols), BF16),
            jax.ShapeDtypeStruct((rows, cols), BF16),
            jax.ShapeDtypeStruct((rows, cols), BF16),
        ),
        in_specs=[hbm, hbm, hbm, hbm, vmem, vmem, hbm, hbm, hbm],
        out_specs=(vmem, vmem, vmem),
        scratch_shapes=[
            pltpu.VMEM((requests // 2, tokens, width), BF16),
            pltpu.VMEM((requests // 2, tokens, width), BF16),
            pltpu.VMEM(mask.shape, jnp.int32),
            pltpu.VMEM((1, width), F32),
            pltpu.VMEM((Z, rows // 2, X * BLK), BF16),
            pltpu.VMEM((Z, X * rows, COVER), BF16),
            pltpu.VMEM((3, Z, COVER, cols), BF16),
            pltpu.VMEM((3, X * rows, cols), F32),
            pltpu.VMEM((3, X - 1, rows, cols), BF16),
            pltpu.VMEM((3, X - 1, rows, cols), BF16),
            pltpu.VMEM((requests, 16, cols), BF16),
            dma((2, 3, Z // 2)),
            dma((2, 3, Z // 2)),
            dma((X - 1,)),
            dma((X - 1,)),
            dma((X,)),
            dma((X,)),
            dma((3, X - 1)),
            dma((3, X - 1)),
            dma((2, Z // 2)),
            dma((2, Z // 2)),
            dma((2, 2, Z)),
            dma((2, 2, Z)),
            dma((9,)),
        ],
        compiler_params=pltpu.CompilerParams(
            collective_id=0, has_side_effects=True, vmem_limit_bytes=24 << 20
        ),
    )(*in_hbm(block_input, accepted, mask, gain), cosine, sine, *in_hbm(w_query, w_key, w_value))


def attend_kernel(
    base,
    lengths_hbm,
    table_hbm,
    q_ref,
    k_ref,
    v_hbm,
    kn_ref,
    vn_ref,
    o_ref,
    st_ref,
    acc,
    stats,
    qt,
    v_ref,
    table_ref,
    lengths,
    owner,
    live,
    sems,
):
    heads = acc.shape[1]
    queries = acc.shape[3]
    scale = HD ** (-0.5)
    loads = [
        pltpu.make_async_copy(lengths_hbm, lengths, sems.at[0]),
        pltpu.make_async_copy(table_hbm, table_ref, sems.at[1]),
        pltpu.make_async_copy(v_hbm, v_ref, sems.at[2]),
    ]
    for copy in loads:
        copy.start()
    stats[...] = jnp.zeros_like(stats)

    key_pass = lax.broadcasted_iota(jnp.int32, (16, queries), 0) // 8
    query_pass = lax.rem(lax.broadcasted_iota(jnp.int32, (16, queries), 1) // 8, 2)
    same = key_pass == query_pass

    @pl.loop(0, q_ref.shape[0])
    def _(r):
        for h in range(heads):
            col = slice(h * HD, (h + 1) * HD)
            qt[r, h] = jnp.transpose(q_ref[r, :, col])
            scores = jnp.dot(kn_ref[r, :, col], qt[r, h], preferred_element_type=F32) * scale
            scores = jnp.where(same, scores, -1e30)
            peak = jnp.max(scores, axis=0, keepdims=True)
            weights = jnp.where(same, jnp.exp(scores - peak), 0.0)
            high = weights.astype(BF16)
            low = (weights - high.astype(F32)).astype(BF16)
            values = vn_ref[r, :, col]
            acc[r, h] = lax.dot_general(
                jnp.concatenate([values, values], axis=0),
                jnp.concatenate([high, low], axis=0),
                TN,
                preferred_element_type=F32,
            )
            stats[pl.ds(r * 8 + h, 1), :] = peak
            stats[pl.ds(r * 8 + 4 + h, 1), :] = jnp.sum(weights, axis=0, keepdims=True)

    for copy in loads:
        copy.wait()
    shape = table_ref.shape
    slots = lax.broadcasted_iota(jnp.int32, shape, 0) * shape[1] + lax.broadcasted_iota(jnp.int32, shape, 1)
    slots = slots.astype(F32)
    for p in range(k_ref.shape[0]):
        found = jnp.sum(jnp.where(table_ref[...] == base[0] + p, slots, 0.0)).astype(jnp.int32)
        owner[p] = found // MAXP
        live[p] = lengths[found // MAXP] - lax.rem(found, MAXP) * PAGE

    slot = lax.broadcasted_iota(jnp.int32, (PAGE, queries), 0)

    @pl.loop(0, k_ref.shape[0])
    def _(p):
        r = owner[p]

        @pl.when(live[p] > 0)
        def _():
            alive = slot < live[p]
            for h in range(heads):
                col = slice(h * HD, (h + 1) * HD)
                scores = jnp.dot(k_ref[p, :, col], qt[r, h], preferred_element_type=F32) * scale
                scores = jnp.where(alive, scores, -1e30)
                page_peak = jnp.max(scores, axis=0, keepdims=True)
                weights = jnp.exp(scores - page_peak)
                page_out = lax.dot_general(
                    v_ref[p, :, col], weights.astype(BF16), TN, preferred_element_type=F32
                )
                m_row = pl.ds(r * 8 + h, 1)
                l_row = pl.ds(r * 8 + 4 + h, 1)
                before = stats[m_row, :]
                after = jnp.maximum(before, page_peak)
                old, new = jnp.exp(before - after), jnp.exp(page_peak - after)
                acc[r, h] = acc[r, h] * old + page_out * new
                stats[m_row, :] = after
                stats[l_row, :] = stats[l_row, :] * old + jnp.sum(weights, axis=0, keepdims=True) * new

    @pl.loop(0, q_ref.shape[0])
    def _(r):
        for h in range(heads):
            o_ref[r, :, h * HD : (h + 1) * HD] = jnp.transpose(acc[r, h].astype(BF16))

    st_ref[...] = jnp.transpose(stats[...])


def attend(base, lengths, page_table, q_all, key_cache, value_cache, new_keys, new_values):
    requests, queries, cols = q_all.shape
    pages = key_cache.shape[0]
    heads = cols // HD
    vmem = pl.BlockSpec(memory_space=pltpu.VMEM)
    smem = pl.BlockSpec(memory_space=pltpu.SMEM)
    hbm = pl.BlockSpec(memory_space=pltpu.HBM)
    return pl.pallas_call(
        attend_kernel,
        name="attend",
        out_shape=(
            jax.ShapeDtypeStruct((requests, queries, cols), BF16),
            jax.ShapeDtypeStruct((queries, 128), F32),
        ),
        in_specs=[smem, hbm, hbm, vmem, vmem, hbm, vmem, vmem],
        out_specs=(vmem, vmem),
        scratch_shapes=[
            pltpu.VMEM((requests, heads, HD, queries), F32),
            pltpu.VMEM((128, queries), F32),
            pltpu.VMEM((requests, heads, HD, queries), BF16),
            pltpu.VMEM(value_cache.shape, BF16),
            pltpu.VMEM(page_table.shape, jnp.int32),
            pltpu.SMEM(lengths.shape, jnp.int32),
            pltpu.SMEM((pages,), jnp.int32),
            pltpu.SMEM((pages,), jnp.int32),
            pltpu.SemaphoreType.DMA((3,)),
        ],
        compiler_params=pltpu.CompilerParams(vmem_limit_bytes=20 << 20),
    )(base, *in_hbm(lengths, page_table), q_all, key_cache, *in_hbm(value_cache), new_keys, new_values)


def join(tables):
    peak = functools.reduce(jnp.maximum, tables)
    factors = [jnp.exp(table - peak) for table in tables]
    total = sum(pltpu.roll(factor, 4, 1) * table for factor, table in zip(factors, tables))
    lane = lax.broadcasted_iota(jnp.int32, peak.shape, 1)
    return jnp.where(lax.rem(lane, 8) >= 4, total, peak), factors


def weigh(factors, sources, r, h):
    lane = r * 8 + h
    return sum(
        factor[:, lane : lane + 1] * source[:, h * HD : (h + 1) * HD].astype(F32)
        for factor, source in zip(factors, sources)
    )


def finish_kernel(
    Z,
    o_ref,
    st_ref,
    wo_ref,
    first_ref,
    second_ref,
    far,
    far_st,
    near,
    near_st,
    pair,
    pair_st,
    both,
    both_st,
    cb,
    cb_st,
    rb,
    rb_st,
    wo_all,
    ctx,
    pb,
    pc,
    mm,
    pm,
    ph,
    ob,
    of,
    ring_send,
    ring_recv,
    x_send,
    x_recv,
    xs_send,
    xs_recv,
    b_send,
    b_recv,
    bs_send,
    bs_recv,
    c_send,
    c_recv,
    d_send,
    d_recv,
    y_send,
    y_recv,
    e_send,
    e_recv,
    local_sem,
):
    seq, head, z, x, at = place(Z)
    requests = o_ref.shape[0]
    heads = o_ref.shape[4] // HD
    ys = Z // 2
    core, y = lax.rem(head, 2), head // 2
    partner = (seq, head + 1 - 2 * core)

    def along_y(d):
        return (seq, lax.rem(y + d, ys) * 2 + core)

    kept = pltpu.make_async_copy(wo_ref, wo_all.at[z // 2, lax.rem(z, 2)], local_sem.at[0])
    kept.start()
    greet(
        [at(d, 0) for d in range(1, Z)]
        + [at(0, d) for d in range(1, X)]
        + [along_y(d) for d in range(1, ys)]
        + [partner]
    )

    def far_off(i):
        return Z // 2 + (1 - 2 * lax.rem(i, 2)) * ((i + 1) // 2)

    def chunk(i):
        return lax.rem(z + far_off(i), Z), 1 - 2 * lax.rem(i, 2)

    def step_x(n):
        return lax.rem(x + n + X, X)

    def send_far(i):
        there, way = chunk(i)
        return (
            remote(o_ref.at[:, there, step_x(2)], far.at[there], x_send.at[0, i], x_recv.at[0, i], at(0, way + X)),
            remote(st_ref.at[there, step_x(2)], far_st.at[there], xs_send.at[0, i], xs_recv.at[0, i], at(0, way + X)),
        )

    def send_near(i):
        there, way = chunk(i)
        to = step_x(-way)
        return (
            remote(o_ref.at[:, there, to], near.at[there], x_send.at[1, i], x_recv.at[1, i], at(0, X - way)),
            remote(st_ref.at[there, to], near_st.at[there], xs_send.at[1, i], xs_recv.at[1, i], at(0, X - way)),
        )

    def send_pair(i):
        there, way = chunk(i)
        return (
            remote(pair.at[there], both.at[there], x_send.at[2, i], x_recv.at[2, i], at(0, way + X)),
            remote(pair_st.at[there], both_st.at[there], xs_send.at[2, i], xs_recv.at[2, i], at(0, way + X)),
        )

    def send_z(i):
        there, _ = chunk(i)
        target = (there * X + x, head)
        return (
            remote(cb.at[there], rb.at[i], b_send.at[i], b_recv.at[i], target),
            remote(cb_st.at[there], rb_st.at[i], bs_send.at[i], bs_recv.at[i], target),
        )

    def ring(right, k, src=None):
        block = lax.rem(z - k + Z, Z) if right else lax.rem(z + k, Z)
        way = 1 if right else 0
        slot = wo_all.at[block // 2, lax.rem(block, 2)]
        return remote(
            slot if src is None else src,
            slot,
            ring_send.at[way, k],
            ring_recv.at[way, k],
            at(1 if right else -1, 0),
        )

    right_steps, left_steps = Z // 2, Z - 1 - Z // 2

    def begin(i):
        for copy in send_far(i) + send_near(i):
            copy.start()

    begin(0)
    begin(1)
    begin(2)
    ring(True, 0, wo_ref).start()
    ring(False, 0, wo_ref).start()
    kept.wait()

    def middle(i):
        there, way = chunk(i)
        for copy in send_far(i):
            copy.wait_recv()
        table, factors = join([st_ref[there, step_x(way)], far_st[there]])
        pair_st[there] = table
        for r in range(requests):
            for h in range(heads):
                value = weigh(factors, [o_ref[r, there, step_x(way)], far[there, r]], r, h)
                pair[there, r, :, h * HD : (h + 1) * HD] = value.astype(BF16)
        for copy in send_pair(i):
            copy.start()

    def end(i):
        there, _ = chunk(i)
        for copy in send_near(i) + send_pair(i):
            copy.wait_recv()
        table, factors = join([st_ref[there, x], near_st[there], both_st[there]])
        cb_st[there] = table
        for r in range(requests):
            for h in range(heads):
                value = weigh(factors, [o_ref[r, there, x], near[there, r], both[there, r]], r, h)
                cb[there, r, :, h * HD : (h + 1) * HD] = value.astype(BF16)

    middle(0)

    @pl.loop(1, Z)
    def _(i):
        @pl.when(i + 2 < Z)
        def _():
            begin(i + 2)

        middle(i)
        end(i - 1)
        for copy in send_z(i - 1):
            copy.start()

        @pl.when(i < right_steps)
        def _():
            ring(True, i - 1).wait_recv()
            ring(True, i).start()

        @pl.when(i < left_steps)
        def _():
            ring(False, i - 1).wait_recv()
            ring(False, i).start()

    end(Z - 1)
    for i in range(Z - 1):
        for copy in send_z(i):
            copy.wait_recv()

    mine = pl.multiple_of(x * 128, 128)
    table, factors = join([cb_st[z]] + [rb_st[i] for i in range(Z - 1)])
    inverse = 1.0 / table

    def share(half, d):
        rows = ctx.at[pl.ds(pl.multiple_of(mine + half * 64, 64), 64)]
        return remote(rows, rows, c_send.at[half, d - 1], c_recv.at[half, d - 1], at(0, d))

    for r in range(requests):
        sources = [cb[z, r]] + [rb[i, r] for i in range(Z - 1)]
        for h in range(heads):
            lane = r * 8 + h + 4
            value = weigh(factors, sources, r, h) * inverse[:, lane : lane + 1]
            ctx[pl.ds(mine + r * 16, 16), h * HD : (h + 1) * HD] = value.astype(BF16)
        if r % 4 == 3:
            for d in (2, 1, 3):
                share(r // 4, d).start()

    shares = [share(half, d) for half in range(2) for d in range(1, X)]
    ring(True, right_steps - 1).wait_recv()
    ring(False, left_steps - 1).wait_recv()
    for copy in shares:
        copy.wait_recv()

    def multiply(c):
        weights = wo_all[:, c].reshape(ys * BLK, ctx.shape[1])
        result = lax.dot_general(weights, ctx[...], NT, preferred_element_type=F32)
        return result.reshape(ys, BLK, ctx.shape[0])

    def to_core(d):
        there = lax.rem(y + d, ys)
        return remote(pb.at[there], pc.at[there], d_send.at[d], d_recv.at[d], partner)

    def to_y(d):
        return remote(pm.at[d - 1], ph.at[d - 1], y_send.at[d - 1], y_recv.at[d - 1], along_y(d))

    pb[...] = multiply(1 - core).astype(BF16)
    for d in (2, 1, 3, 0):
        to_core(d).start()
    mm[...] = multiply(core)
    for d in (2, 1, 3):
        there = lax.rem(y + d, ys)
        to_core(d).wait_recv()
        pm[d - 1] = (mm[there] + pc[there].astype(F32)).astype(BF16)
        to_y(d).start()

    to_core(0).wait_recv()
    total = mm[y] + pc[y].astype(F32)
    for d in range(1, ys):
        to_y(d).wait_recv()
        total = total + ph[d - 1].astype(F32)
    ob[...] = total.astype(BF16)
    block = pl.ds(pl.multiple_of(x * BLK, 32), BLK)

    def to_owner(d):
        there = pl.multiple_of(lax.rem(x + d, X) * 128, 128)
        return remote(ob.at[:, pl.ds(there, 128)], of.at[block], e_send.at[d - 1], e_recv.at[d - 1], at(0, d))

    for d in (2, 1, 3):
        to_owner(d).start()
    last = pltpu.make_async_copy(ob.at[:, pl.ds(mine, 128)], of.at[block], local_sem.at[1])
    last.start()
    last.wait()
    for d in range(1, X):
        to_owner(d).wait_recv()
    result = jnp.transpose(of[...].astype(F32))
    for r in range(requests):
        first_ref[r] = result[r * 16 : r * 16 + 8].astype(BF16)
        second_ref[r] = result[r * 16 + 8 : r * 16 + 16].astype(BF16)

    @pl.loop(0, Z)
    def _(i):
        for copy in send_far(i) + send_near(i) + send_pair(i):
            copy.wait_send()

    for k in range(right_steps):
        ring(True, k).wait_send()
    for k in range(left_steps):
        ring(False, k).wait_send()
    for i in range(Z - 1):
        for copy in send_z(i):
            copy.wait_send()
    for copy in shares:
        copy.wait_send()
    for d in range(1, X):
        to_owner(d).wait_send()
    for d in range(ys):
        to_core(d).wait_send()
    for d in range(1, ys):
        to_y(d).wait_send()


def finish(Z, out, table, w_out, tokens):
    requests = out.shape[0]
    cols = out.shape[4]
    rows = requests * 16
    ys = Z // 2
    vmem = pl.BlockSpec(memory_space=pltpu.VMEM)
    hbm = pl.BlockSpec(memory_space=pltpu.HBM)
    dma = pltpu.SemaphoreType.DMA
    shape = jax.ShapeDtypeStruct((requests, tokens, X * BLK), BF16)
    chunks = pltpu.VMEM((Z, requests, 16, cols), BF16)
    tables = pltpu.VMEM((Z, 16, 128), F32)
    return pl.pallas_call(
        functools.partial(finish_kernel, Z),
        name="finish",
        out_shape=(shape, shape),
        in_specs=[vmem, vmem, hbm],
        out_specs=(vmem, vmem),
        scratch_shapes=[
            chunks,
            tables,
            chunks,
            tables,
            chunks,
            tables,
            chunks,
            tables,
            chunks,
            tables,
            pltpu.VMEM((Z - 1, requests, 16, cols), BF16),
            pltpu.VMEM((Z - 1, 16, 128), F32),
            pltpu.VMEM((ys, 2, BLK, cols), BF16),
            pltpu.VMEM((X * rows, cols), BF16),
            pltpu.VMEM((ys, BLK, X * rows), BF16),
            pltpu.VMEM((ys, BLK, X * rows), BF16),
            pltpu.VMEM((ys, BLK, X * rows), F32),
            pltpu.VMEM((ys - 1, BLK, X * rows), BF16),
            pltpu.VMEM((ys - 1, BLK, X * rows), BF16),
            pltpu.VMEM((BLK, X * rows), BF16),
            pltpu.VMEM((X * BLK, rows), BF16),
            dma((2, Z // 2)),
            dma((2, Z // 2)),
            dma((3, Z)),
            dma((3, Z)),
            dma((3, Z)),
            dma((3, Z)),
            dma((Z - 1,)),
            dma((Z - 1,)),
            dma((Z - 1,)),
            dma((Z - 1,)),
            dma((2, X - 1)),
            dma((2, X - 1)),
            dma((ys,)),
            dma((ys,)),
            dma((ys - 1,)),
            dma((ys - 1,)),
            dma((X - 1,)),
            dma((X - 1,)),
            dma((2,)),
        ],
        compiler_params=pltpu.CompilerParams(
            collective_id=1, has_side_effects=True, vmem_limit_bytes=20 << 20
        ),
    )(out, table, *in_hbm(w_out))


def per_device(
    Z,
    block_input,
    accepted,
    accept_mask,
    cache_lengths,
    page_table,
    norm_gain,
    w_query,
    w_key,
    w_value,
    w_out,
    key_cache,
    value_cache,
):
    seq = lax.axis_index("seq")
    requests, tokens, width = block_input.shape
    half = HD // 2
    frequency = 10000.0 ** (-(jnp.arange(half).astype(F32) * 2.0) / HD)
    positions = (
        cache_lengths[:, None] + seq * tokens + jnp.arange(tokens, dtype=jnp.int32)[None, :]
    ).astype(F32)
    angles = jnp.broadcast_to(positions[:, None, :, None] * frequency, (requests, 2, tokens, half))
    angles = angles.reshape(requests * 2 * tokens, half)
    cosine, sine = jnp.cos(angles), jnp.sin(angles)
    cosine = jnp.concatenate([cosine, cosine], axis=1)
    sine = jnp.concatenate([-sine, sine], axis=1)

    q_all, new_keys, new_values = project(
        Z,
        block_input,
        accepted,
        accept_mask,
        norm_gain.reshape(1, width),
        cosine,
        sine,
        w_query,
        w_key,
        w_value,
    )
    cols = q_all.shape[3]
    queries = Z * X * 16
    out, table = attend(
        (seq * key_cache.shape[0]).astype(jnp.int32).reshape(1),
        cache_lengths,
        page_table.reshape(-1, 128),
        q_all.reshape(requests, queries, cols),
        key_cache,
        value_cache,
        new_keys.reshape(requests, 16, cols),
        new_values.reshape(requests, 16, cols),
    )
    return finish(Z, out.reshape(requests, Z, X, 16, cols), table.reshape(Z, X, 16, 128), w_out, tokens)


def solution(mesh):
    placed = (
        P(None, "seq", None),
        P(None, "seq", None),
        P(None, "seq"),
        P(),
        P(),
        P(),
        P("seq", "head"),
        P("seq", "head"),
        P("seq", "head"),
        P("seq", "head"),
        P("seq", None, "head"),
        P("seq", None, "head"),
    )
    return jax.shard_map(
        functools.partial(per_device, mesh.shape["seq"] // X),
        mesh=mesh,
        in_specs=placed,
        out_specs=(P(None, "seq", "head"), P(None, "seq", "head")),
        check_vma=False,
    )
```

time: 212 us -> 167 us (0.79)
  Pallas kernels: 198 us -> 163 us
  local copies, waits for them, and re-layouts: 10 us -> 1.29 us
    pallas_call x1, Pallas kernels: 99.3 us -> 71.4 us  [project(): pl.pallas_call(functools.partial(project_kernel, Z), name='project', out_...]
    unnamed x20 -> x4, local copies, waits for them, and re-layouts: 9.18 us -> 1.28 us
    pallas_call x1, Pallas kernels: 80.9 us -> 76 us  [finish(): pl.pallas_call(functools.partial(finish_kernel, Z), name='finish', out_sh...]
    pallas_call x1, Pallas kernels: 17.5 us -> 15.1 us  [attend(): pl.pallas_call(attend_kernel, name='attend', out_shape=(jax.ShapeDtypeStr...]
where the time goes in v2:
time: 167 us; the launch traced here: 166 us
  Pallas kernels  163 us (98%)
    pallas_call x1, Pallas kernels, finish(): pl.pallas_call(functools.partial(finish_kernel, Z), name='finish', out_sh...  76 us
    pallas_call x1, Pallas kernels, project(): pl.pallas_call(functools.partial(project_kernel, Z), name='project', out_...  71.4 us
    pallas_call x1, Pallas kernels, attend(): pl.pallas_call(attend_kernel, name='attend', out_shape=(jax.ShapeDtypeStr...  15.1 us

profile of v2, /device:TPU:33, one launch (start us, length us, event | category | flops | bytes accessed | tf_op | source)
XLA Modules:
  0.0 165.7 jit_solution(5841391220231607538)
XLA Ops:
  0.6 0.0 copy-start
  0.6 0.8 broadcast_add_fusion
  1.4 0.1 add_convert_fusion
  1.5 0.2 multiply_sine_fusion
  1.8 0.1 pad_maximum_fusion
  1.9 71.4 %project.1 = (bf16[8,32,16,384]{3,2,1,0:T(8,128)(2,1)S(1)}, bf16[128,384]{1,0:T(8,128)(2,1)S(1)}, bf16[128,384]{1,0:T(8,128)(2,1)S(1)}) custom-call(bf16[8,8,5120]{2,1,0:T(8,128)(2,1)} %x_hbm.1, bf16[8,8,5120]{2,1,0:T(8,128)(2,1)} %a_hbm.1, s32[8,8]{1,0:T(8,128)} %mask_hbm.1, f32[1,5120]{1,0:T(1,128)} %bitcast.18, f32[128,128]{1,0:T(8,128)S(1)} %get-tuple-element.14.cos_ref, ...), custom_call_target="tpu_custom_call" | custom-call | tf_op jit(solution)/shard_map/project/pallas_call | solution.py:321
  73.3 0.0 copy-done
  73.3 15.1 %attend.1 = (bf16[8,512,384]{2,1,0:T(8,128)(2,1)S(1)}, f32[512,128]{1,0:T(8,128)S(1)}) custom-call(s32[1]{0:T(128)} %bitcast.base, s32[8]{0:T(128)} %lengths_hbm.1, s32[4,128]{1,0:T(4,128)} %bitcast.19, bf16[8,512,384]{2,1,0:T(8,128)(2,1)S(1)} %bitcast.11, bf16[16,128,384]{2,1,0:T(8,128)(2,1)S(1)} %copy-done, bf16[16,128,384]{2,1,0:T(8,128)(2,1)} %v_hbm.1, ...), custom_call_target="tpu_custom_call" | custom-call | tf_op jit(solution)/shard_map/attend/pallas_call | solution.py:473
  88.4 76.0 %finish.1 = (bf16[8,8,640]{2,1,0:T(8,128)(2,1)S(1)}, bf16[8,8,640]{2,1,0:T(8,128)(2,1)S(1)}) custom-call(bf16[8,8,4,16,384]{4,3,2,1,0:T(8,128)(2,1)S(1)} %bitcast.12, f32[8,4,16,128]{3,2,1,0:T(8,128)S(1)} %bitcast.13, bf16[160,384]{1,0:T(8,128)(2,1)} %wo_ref.1), custom_call_target="tpu_custom_call" | custom-call | tf_op jit(solution)/shard_map/finish/pallas_call | solution.py:799
  164.4 0.6 copy.16
  165.1 0.6 copy.17
  (4 shorter events, 0.0 us)
Async XLA Ops:
  0.6 72.7 %copy-start = (bf16[16,128,384]{2,1,0:T(8,128)(2,1)S(1)}, bf16[16,128,384]{2,1,0:T(8,128)(2,1)}, u32[]{:S(2)}) copy-start(bf16[16,128,384]{2,1,0:T(8,128)(2,1)} %k_ref.1) | copy-start | bytes 4718596

commit v3 on v2

--- a/solution.py
+++ b/solution.py
@@ -12,6 +12,10 @@
 MAXP = 64
 X = 4
 BLK = 160
+FIRST = 6
+WINDOW = 4
+LAG = 3
+HOLD = 2
 COVER = 256
 MESH = pl.DeviceIdType.MESH
 F32 = jnp.float32
@@ -22,6 +26,17 @@
 
 def in_hbm(*arrays):
     return [pltpu.with_memory_space_constraint(array, pltpu.HBM) for array in arrays]
+
+
+ORDER = (
+    "q1", "q2", "k0", "tf", "q3", "k1", "v0", "th", "mq07", "q4", "mq78", "sq",
+    "k2", "v1", "mk05", "cq", "p0", "k3", "v2", "rx", "p1", "p2", "k4", "mk58",
+    "sk", "v3", "p3", "p4", "v4", "mv08", "sv", "p5", "p6", "p7", "p8", "p9",
+    "ck", "cv",
+)
+
+
+LATE = ("x16", "c0", "x68", "own", "wo", "m0", "c1", "m1", "y0", "y1")
 
 
 def place(Z):
@@ -85,6 +100,8 @@
     zq_recv,
     xq_send,
     xq_recv,
+    rx_send,
+    rx_recv,
     local_sem,
 ):
     seq, head, z, x, at = place(Z)
@@ -128,7 +145,7 @@
                 if k < steps(t, right):
                     ring(right, t, k).start()
 
-    advance((0, 1), 0)
+    advance((0,), 0)
     for copy in loads:
         copy.wait()
 
@@ -179,19 +196,6 @@
                 wb[t, c, pl.ds(stripe, 32), :] = zero
 
     acc[...] = jnp.zeros_like(acc)
-    advance((0, 1), 1)
-    advance((0, 1), 2)
-    for d in (1, 3, 2):
-        token(d).wait_recv()
-        across(d).start()
-    advance((0, 1), 3)
-    advance((2,), 0)
-    own_tokens.wait()
-    for copy in kept:
-        copy.wait()
-    for d in range(X):
-        across(d).wait_recv()
-
     def multiply(t, low, high):
         @pl.loop(low, high)
         def _(j):
@@ -223,39 +227,48 @@
             pieces.append(piece * cos_ref[...] + pltpu.roll(piece, HD // 2, 1) * sin_ref[...])
         return jnp.concatenate(pieces, axis=1).astype(BF16)
 
-    multiply(0, 0, Z - 1)
-    multiply(1, 0, Z - 1)
-    advance((0, 1), 4)
-    multiply(0, Z - 1, Z)
-    spread(0)
-    multiply(1, Z - 1, Z)
-    spread(1)
-    advance((2,), 1)
-    query = turn(collect(0))
-    for r in range(qloc.shape[0]):
-        qloc[r] = query[r * 16 : (r + 1) * 16]
-    own_query = pltpu.make_async_copy(qloc, q_all.at[:, seq], local_sem.at[7])
-    own_query.start()
+    first = pl.ds(0, FIRST)
+    rest = pl.ds(FIRST, qloc.shape[0] - FIRST)
+    hops = {True: Z // 2, False: Z - 1 - Z // 2}
 
     def to_z(right, k):
-        slot = q_all.at[:, (lax.rem(z - k + Z, Z) if right else lax.rem(z + k, Z)) * X + x]
+        slot = q_all.at[first, (lax.rem(z - k + Z, Z) if right else lax.rem(z + k, Z)) * X + x]
         i = 1 if right else 0
         return remote(
-            qloc if k == 0 else slot, slot, zq_send.at[i, k], zq_recv.at[i, k], at(1 if right else -1, 0)
+            qloc.at[first] if k == 0 else slot,
+            slot,
+            zq_send.at[0, i, k],
+            zq_recv.at[0, i, k],
+            at(1 if right else -1, 0),
         )
 
-    hops = {True: Z // 2, False: Z - 1 - Z // 2}
-
     def to_x(dz, way):
-        slot = q_all.at[:, lax.rem(z - dz + Z, Z) * X + x]
+        slot = q_all.at[first, lax.rem(z - dz + Z, Z) * X + x]
         i = (way + 1) // 2
-        return remote(qloc if dz == 0 else slot, slot, xq_send.at[i, 0, dz], xq_recv.at[i, 0, dz], at(0, way + X))
+        return remote(
+            qloc.at[first] if dz == 0 else slot, slot, xq_send.at[i, 0, dz], xq_recv.at[i, 0, dz], at(0, way + X)
+        )
 
     def onward(dz):
         way = 1 - 2 * (dz % 2)
-        slot = q_all.at[:, lax.rem(z - dz + Z, Z) * X + lax.rem(x - way + X, X)]
+        slot = q_all.at[first, lax.rem(z - dz + Z, Z) * X + lax.rem(x - way + X, X)]
         i = (way + 1) // 2
         return remote(slot, slot, xq_send.at[i, 1, dz], xq_recv.at[i, 1, dz], at(0, way + X))
+
+    def rest_x(d):
+        return remote(qloc.at[rest], q_all.at[rest, seq], rx_send.at[d - 1], rx_recv.at[d - 1], at(0, d))
+
+    def rest_z(right, k):
+        block = lax.rem(z - k + Z, Z) if right else lax.rem(z + k, Z)
+        slot = q_all.at[rest, pl.ds(block * X, X)]
+        i = 1 if right else 0
+        return remote(slot, slot, zq_send.at[1, i, k], zq_recv.at[1, i, k], at(1 if right else -1, 0))
+
+    def rest_step(right, k):
+        if 0 < k <= hops[right]:
+            rest_z(right, k - 1).wait_recv()
+        if 0 <= k < hops[right]:
+            rest_z(right, k).start()
 
     arrival = [0] + sorted(range(1, Z), key=lambda d: min(d, Z - d))
 
@@ -269,27 +282,71 @@
                     to_z(right, k - 1).wait_recv()
                     if k < hops[right]:
                         to_z(right, k).start()
+                    rest_step(right, k - 1)
                 to_x(dz, 1).start()
                 to_x(dz, -1).start()
-            if i > 0:
-                dz = arrival[i - 1]
+            if i >= HOLD:
+                dz = arrival[i - HOLD]
                 to_x(dz, 1 - 2 * (dz % 2)).wait_recv()
                 onward(dz).start()
 
-    to_z(True, 0).start()
-    to_z(False, 0).start()
-    pass_on(0, 1)
-    advance((2,), 2)
-    kn_ref[...] = turn(collect(1))
-    advance((2,), 3)
-    pass_on(1, 3)
-    advance((2,), 4)
-    multiply(2, 0, Z)
-    spread(2)
-    pass_on(3, Z + 1)
-    vn_ref[...] = collect(2).astype(BF16)
-
-    own_query.wait()
+    own_query = pltpu.make_async_copy(qloc, q_all.at[:, seq], local_sem.at[7])
+
+    def forward_tokens():
+        for d in (1, 3, 2):
+            token(d).wait_recv()
+            across(d).start()
+
+    def have_tokens():
+        own_tokens.wait()
+        for copy in kept:
+            copy.wait()
+        for d in range(X):
+            across(d).wait_recv()
+
+    def query_ready():
+        query = turn(collect(0))
+        for r in range(qloc.shape[0]):
+            qloc[r] = query[r * 16 : (r + 1) * 16]
+        to_z(True, 0).start()
+        to_z(False, 0).start()
+        for d in (2, 1, 3):
+            rest_x(d).start()
+        own_query.start()
+
+    def have_rest():
+        own_query.wait()
+        for d in range(1, X):
+            rest_x(d).wait_recv()
+
+    def key_ready():
+        kn_ref[...] = turn(collect(1))
+
+    def value_ready():
+        vn_ref[...] = collect(2).astype(BF16)
+
+    named = {
+        "tf": forward_tokens,
+        "th": have_tokens,
+        "cq": query_ready,
+        "rx": have_rest,
+        "ck": key_ready,
+        "cv": value_ready,
+    }
+    for word in ORDER:
+        if word in named:
+            named[word]()
+        elif word[0] == "m":
+            multiply("qkv".index(word[1]), int(word[2]), int(word[3]))
+        elif word[0] == "s":
+            spread("qkv".index(word[1]))
+        elif word[0] == "p":
+            pass_on(int(word[1]), int(word[1]) + 1)
+        else:
+            advance(("qkv".index(word[0]),), int(word[1]))
+    rest_step(False, hops[False])
+    rest_step(True, hops[True])
+
     for t in range(3):
         for right in (True, False):
             for k in range(steps(t, right)):
@@ -303,6 +360,9 @@
     for right in (True, False):
         for k in range(hops[right]):
             to_z(right, k).wait_send()
+            rest_z(right, k).wait_send()
+    for d in range(1, X):
+        rest_x(d).wait_send()
     for dz in range(Z):
         forwarded = 1 - 2 * (dz % 2)
         to_x(dz, -forwarded).wait_recv()
@@ -348,10 +408,12 @@
             dma((X,)),
             dma((3, X - 1)),
             dma((3, X - 1)),
-            dma((2, Z // 2)),
-            dma((2, Z // 2)),
+            dma((2, 2, Z // 2)),
+            dma((2, 2, Z // 2)),
             dma((2, 2, Z)),
             dma((2, 2, Z)),
+            dma((X - 1,)),
+            dma((X - 1,)),
             dma((9,)),
         ],
         compiler_params=pltpu.CompilerParams(
@@ -561,6 +623,7 @@
     seq, head, z, x, at = place(Z)
     requests = o_ref.shape[0]
     heads = o_ref.shape[4] // HD
+    span = requests // 2
     ys = Z // 2
     core, y = lax.rem(head, 2), head // 2
     partner = (seq, head + 1 - 2 * core)
@@ -586,35 +649,39 @@
     def step_x(n):
         return lax.rem(x + n + X, X)
 
-    def send_far(i):
+    def rows_of(half):
+        return pl.ds(half * span, span)
+
+    def send(kind, half, i, src, dst, table_src, table_dst, target):
+        copies = [remote(src, dst, x_send.at[kind, half, i], x_recv.at[kind, half, i], target)]
+        if half == 0:
+            copies.append(remote(table_src, table_dst, xs_send.at[kind, i], xs_recv.at[kind, i], target))
+        return copies
+
+    def send_far(half, i):
         there, way = chunk(i)
-        return (
-            remote(o_ref.at[:, there, step_x(2)], far.at[there], x_send.at[0, i], x_recv.at[0, i], at(0, way + X)),
-            remote(st_ref.at[there, step_x(2)], far_st.at[there], xs_send.at[0, i], xs_recv.at[0, i], at(0, way + X)),
-        )
-
-    def send_near(i):
+        to = step_x(2)
+        src = o_ref.at[rows_of(half), there, to]
+        return send(0, half, i, src, far.at[half, there], st_ref.at[there, to], far_st.at[there], at(0, way + X))
+
+    def send_near(half, i):
         there, way = chunk(i)
         to = step_x(-way)
-        return (
-            remote(o_ref.at[:, there, to], near.at[there], x_send.at[1, i], x_recv.at[1, i], at(0, X - way)),
-            remote(st_ref.at[there, to], near_st.at[there], xs_send.at[1, i], xs_recv.at[1, i], at(0, X - way)),
-        )
-
-    def send_pair(i):
+        src = o_ref.at[rows_of(half), there, to]
+        return send(1, half, i, src, near.at[half, there], st_ref.at[there, to], near_st.at[there], at(0, X - way))
+
+    def send_pair(half, i):
         there, way = chunk(i)
-        return (
-            remote(pair.at[there], both.at[there], x_send.at[2, i], x_recv.at[2, i], at(0, way + X)),
-            remote(pair_st.at[there], both_st.at[there], xs_send.at[2, i], xs_recv.at[2, i], at(0, way + X)),
-        )
-
-    def send_z(i):
+        src, dst = pair.at[half, there], both.at[half, there]
+        return send(2, half, i, src, dst, pair_st.at[there], both_st.at[there], at(0, way + X))
+
+    def send_z(half, i):
         there, _ = chunk(i)
         target = (there * X + x, head)
-        return (
-            remote(cb.at[there], rb.at[i], b_send.at[i], b_recv.at[i], target),
-            remote(cb_st.at[there], rb_st.at[i], bs_send.at[i], bs_recv.at[i], target),
-        )
+        copies = [remote(cb.at[half, there], rb.at[half, i], b_send.at[half, i], b_recv.at[half, i], target)]
+        if half == 0:
+            copies.append(remote(cb_st.at[there], rb_st.at[i], bs_send.at[i], bs_recv.at[i], target))
+        return copies
 
     def ring(right, k, src=None):
         block = lax.rem(z - k + Z, Z) if right else lax.rem(z + k, Z)
@@ -630,53 +697,69 @@
 
     right_steps, left_steps = Z // 2, Z - 1 - Z // 2
 
-    def begin(i):
-        for copy in send_far(i) + send_near(i):
+    def begin(half, i):
+        for copy in send_far(half, i) + send_near(half, i):
             copy.start()
 
-    begin(0)
-    begin(1)
-    begin(2)
+    for i in range(WINDOW + 1):
+        begin(0, i)
     ring(True, 0, wo_ref).start()
     ring(False, 0, wo_ref).start()
     kept.wait()
 
-    def middle(i):
+    def middle(half, i):
         there, way = chunk(i)
-        for copy in send_far(i):
+        for copy in send_far(half, i):
             copy.wait_recv()
         table, factors = join([st_ref[there, step_x(way)], far_st[there]])
-        pair_st[there] = table
-        for r in range(requests):
+        if half == 0:
+            pair_st[there] = table
+        for r in range(span):
+            sources = [o_ref[half * span + r, there, step_x(way)], far[half, there, r]]
             for h in range(heads):
-                value = weigh(factors, [o_ref[r, there, step_x(way)], far[there, r]], r, h)
-                pair[there, r, :, h * HD : (h + 1) * HD] = value.astype(BF16)
-        for copy in send_pair(i):
+                value = weigh(factors, sources, half * span + r, h)
+                pair[half, there, r, :, h * HD : (h + 1) * HD] = value.astype(BF16)
+        for copy in send_pair(half, i):
             copy.start()
 
-    def end(i):
+    def end(half, i):
         there, _ = chunk(i)
-        for copy in send_near(i) + send_pair(i):
+        for copy in send_near(half, i) + send_pair(half, i):
             copy.wait_recv()
         table, factors = join([st_ref[there, x], near_st[there], both_st[there]])
-        cb_st[there] = table
-        for r in range(requests):
+        if half == 0:
+            cb_st[there] = table
+        for r in range(span):
+            sources = [o_ref[half * span + r, there, x], near[half, there, r], both[half, there, r]]
             for h in range(heads):
-                value = weigh(factors, [o_ref[r, there, x], near[there, r], both[there, r]], r, h)
-                cb[there, r, :, h * HD : (h + 1) * HD] = value.astype(BF16)
-
-    middle(0)
+                value = weigh(factors, sources, half * span + r, h)
+                cb[half, there, r, :, h * HD : (h + 1) * HD] = value.astype(BF16)
+
+    def closing(half, i):
+        end(half, i)
+
+        @pl.when(i < Z - 1)
+        def _():
+            for copy in send_z(half, i):
+                copy.start()
+
+    middle(0, 0)
 
     @pl.loop(1, Z)
     def _(i):
-        @pl.when(i + 2 < Z)
+        @pl.when(i + WINDOW < Z)
         def _():
-            begin(i + 2)
-
-        middle(i)
-        end(i - 1)
-        for copy in send_z(i - 1):
-            copy.start()
+            begin(0, i + WINDOW)
+
+        @pl.when(i + WINDOW >= Z)
+        def _():
+            begin(1, i + WINDOW - Z)
+
+        middle(0, i)
+
+        @pl.when(i >= LAG)
+        def _():
+            closing(0, i - LAG)
 
         @pl.when(i < right_steps)
         def _():
@@ -688,63 +771,106 @@
             ring(False, i - 1).wait_recv()
             ring(False, i).start()
 
-    end(Z - 1)
-    for i in range(Z - 1):
-        for copy in send_z(i):
-            copy.wait_recv()
-
-    mine = pl.multiple_of(x * 128, 128)
-    table, factors = join([cb_st[z]] + [rb_st[i] for i in range(Z - 1)])
-    inverse = 1.0 / table
+    begin(1, WINDOW)
+    middle(1, 0)
+    closing(0, Z - LAG)
+
+    def second(low, high):
+        @pl.loop(low, high)
+        def _(i):
+            @pl.when(i + WINDOW < Z)
+            def _():
+                begin(1, i + WINDOW)
+
+            middle(1, i)
+
+            @pl.when(i < LAG)
+            def _():
+                closing(0, Z + i - LAG)
+
+            @pl.when(i >= LAG)
+            def _():
+                closing(1, i - LAG)
+
+    mine = pl.multiple_of(x * (16 * span), 16 * span)
 
     def share(half, d):
-        rows = ctx.at[pl.ds(pl.multiple_of(mine + half * 64, 64), 64)]
+        rows = ctx.at[half, pl.ds(mine, 16 * span)]
         return remote(rows, rows, c_send.at[half, d - 1], c_recv.at[half, d - 1], at(0, d))
 
-    for r in range(requests):
-        sources = [cb[z, r]] + [rb[i, r] for i in range(Z - 1)]
-        for h in range(heads):
-            lane = r * 8 + h + 4
-            value = weigh(factors, sources, r, h) * inverse[:, lane : lane + 1]
-            ctx[pl.ds(mine + r * 16, 16), h * HD : (h + 1) * HD] = value.astype(BF16)
-        if r % 4 == 3:
-            for d in (2, 1, 3):
-                share(r // 4, d).start()
-
-    shares = [share(half, d) for half in range(2) for d in range(1, X)]
-    ring(True, right_steps - 1).wait_recv()
-    ring(False, left_steps - 1).wait_recv()
-    for copy in shares:
-        copy.wait_recv()
-
-    def multiply(c):
-        weights = wo_all[:, c].reshape(ys * BLK, ctx.shape[1])
-        result = lax.dot_general(weights, ctx[...], NT, preferred_element_type=F32)
-        return result.reshape(ys, BLK, ctx.shape[0])
-
-    def to_core(d):
+    def settle(half):
+        for i in range(Z - 1):
+            for copy in send_z(half, i):
+                copy.wait_recv()
+        table, factors = join([cb_st[z]] + [rb_st[i] for i in range(Z - 1)])
+        inverse = 1.0 / table
+        for r in range(span):
+            sources = [cb[half, z, r]] + [rb[half, i, r] for i in range(Z - 1)]
+            for h in range(heads):
+                lane = (half * span + r) * 8 + h
+                value = weigh(factors, sources, half * span + r, h) * inverse[:, lane + 4 : lane + 5]
+                ctx[half, pl.ds(mine + r * 16, 16), h * HD : (h + 1) * HD] = value.astype(BF16)
+        for d in (2, 1, 3):
+            share(half, d).start()
+
+    def multiply(half, c):
+        weights = wo_all[:, c].reshape(ys * BLK, ctx.shape[2])
+        result = lax.dot_general(weights, ctx[half], NT, preferred_element_type=F32)
+        return result.reshape(ys, BLK, ctx.shape[1])
+
+    def to_core(half, d):
         there = lax.rem(y + d, ys)
-        return remote(pb.at[there], pc.at[there], d_send.at[d], d_recv.at[d], partner)
-
-    def to_y(d):
-        return remote(pm.at[d - 1], ph.at[d - 1], y_send.at[d - 1], y_recv.at[d - 1], along_y(d))
-
-    pb[...] = multiply(1 - core).astype(BF16)
-    for d in (2, 1, 3, 0):
-        to_core(d).start()
-    mm[...] = multiply(core)
-    for d in (2, 1, 3):
-        there = lax.rem(y + d, ys)
-        to_core(d).wait_recv()
-        pm[d - 1] = (mm[there] + pc[there].astype(F32)).astype(BF16)
-        to_y(d).start()
-
-    to_core(0).wait_recv()
-    total = mm[y] + pc[y].astype(F32)
-    for d in range(1, ys):
-        to_y(d).wait_recv()
-        total = total + ph[d - 1].astype(F32)
-    ob[...] = total.astype(BF16)
+        return remote(pb.at[half, there], pc.at[half, there], d_send.at[half, d], d_recv.at[half, d], partner)
+
+    def to_y(half, d):
+        return remote(
+            pm.at[half, d - 1], ph.at[half, d - 1], y_send.at[half, d - 1], y_recv.at[half, d - 1], along_y(d)
+        )
+
+    def outputs(half):
+        for d in range(1, X):
+            share(half, d).wait_recv()
+        pb[half] = multiply(half, 1 - core).astype(BF16)
+        for d in (2, 1, 3, 0):
+            to_core(half, d).start()
+        mm[half] = multiply(half, core)
+
+    def spread(half):
+        for d in (2, 1, 3):
+            there = lax.rem(y + d, ys)
+            to_core(half, d).wait_recv()
+            pm[half, d - 1] = (mm[half, there] + pc[half, there].astype(F32)).astype(BF16)
+            to_y(half, d).start()
+
+    def total(half):
+        to_core(half, 0).wait_recv()
+        value = mm[half, y] + pc[half, y].astype(F32)
+        for d in range(1, ys):
+            to_y(half, d).wait_recv()
+            value = value + ph[half, d - 1].astype(F32)
+        return value
+
+    for word in LATE:
+        if word[0] == "x":
+            second(int(word[1]), int(word[2]))
+        elif word == "own":
+
+            @pl.loop(Z - LAG, Z)
+            def _(i):
+                closing(1, i)
+
+        elif word == "wo":
+            ring(True, right_steps - 1).wait_recv()
+            ring(False, left_steps - 1).wait_recv()
+        else:
+            {"c": settle, "m": outputs, "y": spread}[word[0]](int(word[1]))
+    early, late = total(0), total(1)
+    low = lax.broadcasted_iota(jnp.int32, (BLK, 128), 1) < 64
+    for t in range(X // 2):
+        a, b = early[:, t * 128 : (t + 1) * 128], late[:, t * 128 : (t + 1) * 128]
+        ob[:, t * 256 : t * 256 + 128] = jnp.where(low, a, pltpu.roll(b, 64, 1)).astype(BF16)
+        ob[:, t * 256 + 128 : t * 256 + 256] = jnp.where(low, pltpu.roll(a, 64, 1), b).astype(BF16)
+    column = pl.multiple_of(x * 128, 128)
     block = pl.ds(pl.multiple_of(x * BLK, 32), BLK)
 
     def to_owner(d):
@@ -753,7 +879,7 @@
 
     for d in (2, 1, 3):
         to_owner(d).start()
-    last = pltpu.make_async_copy(ob.at[:, pl.ds(mine, 128)], of.at[block], local_sem.at[1])
+    last = pltpu.make_async_copy(ob.at[:, pl.ds(column, 128)], of.at[block], local_sem.at[1])
     last.start()
     last.wait()
     for d in range(1, X):
@@ -763,26 +889,27 @@
         first_ref[r] = result[r * 16 : r * 16 + 8].astype(BF16)
         second_ref[r] = result[r * 16 + 8 : r * 16 + 16].astype(BF16)
 
-    @pl.loop(0, Z)
-    def _(i):
-        for copy in send_far(i) + send_near(i) + send_pair(i):
-            copy.wait_send()
-
+    for half in range(2):
+        @pl.loop(0, Z)
+        def _(i):
+            for copy in send_far(half, i) + send_near(half, i) + send_pair(half, i):
+                copy.wait_send()
+
+        for i in range(Z - 1):
+            for copy in send_z(half, i):
+                copy.wait_send()
+        for d in range(1, X):
+            share(half, d).wait_send()
+        for d in range(ys):
+            to_core(half, d).wait_send()
+        for d in range(1, ys):
+            to_y(half, d).wait_send()
     for k in range(right_steps):
         ring(True, k).wait_send()
     for k in range(left_steps):
         ring(False, k).wait_send()
-    for i in range(Z - 1):
-        for copy in send_z(i):
-            copy.wait_send()
-    for copy in shares:
-        copy.wait_send()
     for d in range(1, X):
         to_owner(d).wait_send()
-    for d in range(ys):
-        to_core(d).wait_send()
-    for d in range(1, ys):
-        to_y(d).wait_send()
 
 
 def finish(Z, out, table, w_out, tokens):
@@ -794,7 +921,7 @@
     hbm = pl.BlockSpec(memory_space=pltpu.HBM)
     dma = pltpu.SemaphoreType.DMA
     shape = jax.ShapeDtypeStruct((requests, tokens, X * BLK), BF16)
-    chunks = pltpu.VMEM((Z, requests, 16, cols), BF16)
+    chunks = pltpu.VMEM((2, Z, requests // 2, 16, cols), BF16)
     tables = pltpu.VMEM((Z, 16, 128), F32)
     return pl.pallas_call(
         functools.partial(finish_kernel, Z),
@@ -813,33 +940,33 @@
             tables,
             chunks,
             tables,
-            pltpu.VMEM((Z - 1, requests, 16, cols), BF16),
+            pltpu.VMEM((2, Z - 1, requests // 2, 16, cols), BF16),
             pltpu.VMEM((Z - 1, 16, 128), F32),
             pltpu.VMEM((ys, 2, BLK, cols), BF16),
-            pltpu.VMEM((X * rows, cols), BF16),
-            pltpu.VMEM((ys, BLK, X * rows), BF16),
-            pltpu.VMEM((ys, BLK, X * rows), BF16),
-            pltpu.VMEM((ys, BLK, X * rows), F32),
-            pltpu.VMEM((ys - 1, BLK, X * rows), BF16),
-            pltpu.VMEM((ys - 1, BLK, X * rows), BF16),
+            pltpu.VMEM((2, X * rows // 2, cols), BF16),
+            pltpu.VMEM((2, ys, BLK, X * rows // 2), BF16),
+            pltpu.VMEM((2, ys, BLK, X * rows // 2), BF16),
+            pltpu.VMEM((2, ys, BLK, X * rows // 2), F32),
+            pltpu.VMEM((2, ys - 1, BLK, X * rows // 2), BF16),
+            pltpu.VMEM((2, ys - 1, BLK, X * rows // 2), BF16),
             pltpu.VMEM((BLK, X * rows), BF16),
             pltpu.VMEM((X * BLK, rows), BF16),
             dma((2, Z // 2)),
             dma((2, Z // 2)),
+            dma((3, 2, Z)),
+            dma((3, 2, Z)),
             dma((3, Z)),
             dma((3, Z)),
-            dma((3, Z)),
-            dma((3, Z)),
-            dma((Z - 1,)),
-            dma((Z - 1,)),
+            dma((2, Z - 1)),
+            dma((2, Z - 1)),
             dma((Z - 1,)),
             dma((Z - 1,)),
             dma((2, X - 1)),
             dma((2, X - 1)),
-            dma((ys,)),
-            dma((ys,)),
-            dma((ys - 1,)),
-            dma((ys - 1,)),
+            dma((2, ys)),
+            dma((2, ys)),
+            dma((2, ys - 1)),
+            dma((2, ys - 1)),
             dma((X - 1,)),
             dma((X - 1,)),
             dma((2,)),

time: 167 us -> 153 us (0.916)
  Pallas kernels: 163 us -> 147 us
    pallas_call x1, Pallas kernels: 76 us -> 67.6 us  [finish(): pl.pallas_call(functools.partial(finish_kernel, Z), name='finish', out_sh...]
    pallas_call x1, Pallas kernels: 71.4 us -> 65.3 us  [project(): pl.pallas_call(functools.partial(project_kernel, Z), name='project', out_...]
where the time goes in v3:
time: 153 us; the launch traced here: 150 us
  Pallas kernels  147 us (96%)
    pallas_call x1, Pallas kernels, finish(): pl.pallas_call(functools.partial(finish_kernel, Z), name='finish', out_sh...  67.6 us
    pallas_call x1, Pallas kernels, project(): pl.pallas_call(functools.partial(project_kernel, Z), name='project', out_...  65.3 us
    pallas_call x1, Pallas kernels, attend(): pl.pallas_call(attend_kernel, name='attend', out_shape=(jax.ShapeDtypeStr...  14.2 us

profile of v3, /device:TPU:33, one launch (start us, length us, event | category | flops | bytes accessed | tf_op | source)
XLA Modules:
  0.0 150.3 jit_solution(7395142766354947255)
XLA Ops:
  0.6 0.0 copy-start
  0.6 0.8 broadcast_add_fusion
  1.4 0.1 add_convert_fusion
  1.5 0.2 multiply_sine_fusion
  1.8 0.1 pad_maximum_fusion
  1.9 65.3 %project.1 = (bf16[8,32,16,384]{3,2,1,0:T(8,128)(2,1)S(1)}, bf16[128,384]{1,0:T(8,128)(2,1)S(1)}, bf16[128,384]{1,0:T(8,128)(2,1)S(1)}) custom-call(bf16[8,8,5120]{2,1,0:T(8,128)(2,1)} %x_hbm.1, bf16[8,8,5120]{2,1,0:T(8,128)(2,1)} %a_hbm.1, s32[8,8]{1,0:T(8,128)} %mask_hbm.1, f32[1,5120]{1,0:T(1,128)} %bitcast.18, f32[128,128]{1,0:T(8,128)S(1)} %get-tuple-element.14.cos_ref, ...), custom_call_target="tpu_custom_call" | custom-call | tf_op jit(solution)/shard_map/project/pallas_call | solution.py:381
  67.2 0.0 copy-done
  67.2 14.2 %attend.1 = (bf16[8,512,384]{2,1,0:T(8,128)(2,1)S(1)}, f32[512,128]{1,0:T(8,128)S(1)}) custom-call(s32[1]{0:T(128)} %bitcast.base, s32[8]{0:T(128)} %lengths_hbm.1, s32[4,128]{1,0:T(4,128)} %bitcast.19, bf16[8,512,384]{2,1,0:T(8,128)(2,1)S(1)} %bitcast.11, bf16[16,128,384]{2,1,0:T(8,128)(2,1)S(1)} %copy-done, bf16[16,128,384]{2,1,0:T(8,128)(2,1)} %v_hbm.1, ...), custom_call_target="tpu_custom_call" | custom-call | tf_op jit(solution)/shard_map/attend/pallas_call | solution.py:535
  81.4 67.6 %finish.1 = (bf16[8,8,640]{2,1,0:T(8,128)(2,1)S(1)}, bf16[8,8,640]{2,1,0:T(8,128)(2,1)S(1)}) custom-call(bf16[8,8,4,16,384]{4,3,2,1,0:T(8,128)(2,1)S(1)} %bitcast.12, f32[8,4,16,128]{3,2,1,0:T(8,128)S(1)} %bitcast.13, bf16[160,384]{1,0:T(8,128)(2,1)} %wo_ref.1), custom_call_target="tpu_custom_call" | custom-call | tf_op jit(solution)/shard_map/finish/pallas_call | solution.py:926
  149.0 0.6 copy.16
  149.6 0.6 copy.17
  (4 shorter events, 0.0 us)
Async XLA Ops:
  0.6 66.6 %copy-start = (bf16[16,128,384]{2,1,0:T(8,128)(2,1)S(1)}, bf16[16,128,384]{2,1,0:T(8,128)(2,1)}, u32[]{:S(2)}) copy-start(bf16[16,128,384]{2,1,0:T(8,128)(2,1)} %k_ref.1) | copy-start | bytes 4718596

commit v4 on v3

--- a/solution.py
+++ b/solution.py
@@ -16,6 +16,9 @@
 WINDOW = 4
 LAG = 3
 HOLD = 2
+PARTS = 2
+UNROLL = 4
+PAIR = 2
 COVER = 256
 MESH = pl.DeviceIdType.MESH
 F32 = jnp.float32
@@ -125,27 +128,27 @@
         copy.start()
     greet([at(d, 0) for d in range(1, Z)] + [at(0, d) for d in range(1, X)] + [partner])
 
-    def ring(right, t, k):
+    def ring(right, t, k, bit):
         block = lax.rem(z - k + Z, Z) if right else lax.rem(z + k, Z)
-        slot = wb.at[t, block, pl.ds(off, BLK)]
-        src = own[t] if k == 0 else slot
+        size = BLK // PARTS
+        slot = wb.at[t, block, pl.ds(pl.multiple_of(off + bit * size, 16), size)]
+        src = own[t].at[pl.ds(bit * size, size)] if k == 0 else slot
         way = 1 if right else 0
-        return remote(
-            src, slot, ring_send.at[way, t, k], ring_recv.at[way, t, k], at(1 if right else -1, 0)
-        )
+        send, recv = ring_send.at[way, t, k, bit], ring_recv.at[way, t, k, bit]
+        return remote(src, slot, send, recv, at(1 if right else -1, 0))
 
     def steps(t, right):
         return Z // 2 if right == (t % 2 == 0) else Z - 1 - Z // 2
 
-    def advance(tensors, k):
-        for t in tensors:
+    def advance(t, k):
+        for bit in range(PARTS):
             for right in (True, False):
                 if 0 < k <= steps(t, right):
-                    ring(right, t, k - 1).wait_recv()
+                    ring(right, t, k - 1, bit).wait_recv()
                 if k < steps(t, right):
-                    ring(right, t, k).start()
-
-    advance((0,), 0)
+                    ring(right, t, k, bit).start()
+
+    advance(0, 0)
     for copy in loads:
         copy.wait()
 
@@ -343,14 +346,15 @@
         elif word[0] == "p":
             pass_on(int(word[1]), int(word[1]) + 1)
         else:
-            advance(("qkv".index(word[0]),), int(word[1]))
+            advance("qkv".index(word[0]), int(word[1]))
     rest_step(False, hops[False])
     rest_step(True, hops[True])
 
     for t in range(3):
         for right in (True, False):
             for k in range(steps(t, right)):
-                ring(right, t, k).wait_send()
+                for bit in range(PARTS):
+                    ring(right, t, k, bit).wait_send()
         for d in range(1, X):
             piece(t, d).wait_send()
     for d in range(1, X):
@@ -400,8 +404,8 @@
             pltpu.VMEM((3, X - 1, rows, cols), BF16),
             pltpu.VMEM((3, X - 1, rows, cols), BF16),
             pltpu.VMEM((requests, 16, cols), BF16),
-            dma((2, 3, Z // 2)),
-            dma((2, 3, Z // 2)),
+            dma((2, 3, Z // 2, PARTS)),
+            dma((2, 3, Z // 2, PARTS)),
             dma((X - 1,)),
             dma((X - 1,)),
             dma((X,)),
@@ -439,6 +443,7 @@
     v_ref,
     table_ref,
     lengths,
+    page,
     owner,
     live,
     sems,
@@ -459,8 +464,7 @@
     query_pass = lax.rem(lax.broadcasted_iota(jnp.int32, (16, queries), 1) // 8, 2)
     same = key_pass == query_pass
 
-    @pl.loop(0, q_ref.shape[0])
-    def _(r):
+    def block_part(r):
         for h in range(heads):
             col = slice(h * HD, (h + 1) * HD)
             qt[r, h] = jnp.transpose(q_ref[r, :, col])
@@ -480,42 +484,53 @@
             stats[pl.ds(r * 8 + h, 1), :] = peak
             stats[pl.ds(r * 8 + 4 + h, 1), :] = jnp.sum(weights, axis=0, keepdims=True)
 
+    @pl.loop(0, q_ref.shape[0] // UNROLL)
+    def _(i):
+        for j in range(UNROLL):
+            block_part(i * UNROLL + j)
+
     for copy in loads:
         copy.wait()
     shape = table_ref.shape
     slots = lax.broadcasted_iota(jnp.int32, shape, 0) * shape[1] + lax.broadcasted_iota(jnp.int32, shape, 1)
     slots = slots.astype(F32)
+    count = jnp.int32(0)
     for p in range(k_ref.shape[0]):
         found = jnp.sum(jnp.where(table_ref[...] == base[0] + p, slots, 0.0)).astype(jnp.int32)
-        owner[p] = found // MAXP
-        live[p] = lengths[found // MAXP] - lax.rem(found, MAXP) * PAGE
+        alive = lengths[found // MAXP] - lax.rem(found, MAXP) * PAGE
+        page[count] = p
+        owner[count] = found // MAXP
+        live[count] = alive
+        count = count + jnp.where(alive > 0, 1, 0)
+    page[count] = 0
+    owner[count] = 0
+    live[count] = 0
 
     slot = lax.broadcasted_iota(jnp.int32, (PAGE, queries), 0)
 
-    @pl.loop(0, k_ref.shape[0])
-    def _(p):
-        r = owner[p]
-
-        @pl.when(live[p] > 0)
-        def _():
-            alive = slot < live[p]
-            for h in range(heads):
-                col = slice(h * HD, (h + 1) * HD)
-                scores = jnp.dot(k_ref[p, :, col], qt[r, h], preferred_element_type=F32) * scale
-                scores = jnp.where(alive, scores, -1e30)
-                page_peak = jnp.max(scores, axis=0, keepdims=True)
-                weights = jnp.exp(scores - page_peak)
-                page_out = lax.dot_general(
-                    v_ref[p, :, col], weights.astype(BF16), TN, preferred_element_type=F32
-                )
-                m_row = pl.ds(r * 8 + h, 1)
-                l_row = pl.ds(r * 8 + 4 + h, 1)
-                before = stats[m_row, :]
-                after = jnp.maximum(before, page_peak)
-                old, new = jnp.exp(before - after), jnp.exp(page_peak - after)
-                acc[r, h] = acc[r, h] * old + page_out * new
-                stats[m_row, :] = after
-                stats[l_row, :] = stats[l_row, :] * old + jnp.sum(weights, axis=0, keepdims=True) * new
+    def page_part(n):
+        p, r = page[n], owner[n]
+        alive = slot < live[n]
+        for h in range(heads):
+            col = slice(h * HD, (h + 1) * HD)
+            scores = jnp.dot(k_ref[p, :, col], qt[r, h], preferred_element_type=F32) * scale
+            scores = jnp.where(alive, scores, -1e30)
+            page_peak = jnp.max(scores, axis=0, keepdims=True)
+            weights = jnp.exp(scores - page_peak)
+            page_out = lax.dot_general(v_ref[p, :, col], weights.astype(BF16), TN, preferred_element_type=F32)
+            m_row = pl.ds(r * 8 + h, 1)
+            l_row = pl.ds(r * 8 + 4 + h, 1)
+            before = stats[m_row, :]
+            after = jnp.maximum(before, page_peak)
+            old, new = jnp.exp(before - after), jnp.exp(page_peak - after)
+            acc[r, h] = acc[r, h] * old + page_out * new
+            stats[m_row, :] = after
+            stats[l_row, :] = stats[l_row, :] * old + jnp.sum(weights, axis=0, keepdims=True) * new
+
+    @pl.loop(0, (count + PAIR - 1) // PAIR)
+    def _(i):
+        for j in range(PAIR):
+            page_part(i * PAIR + j)
 
     @pl.loop(0, q_ref.shape[0])
     def _(r):
@@ -548,8 +563,9 @@
             pltpu.VMEM(value_cache.shape, BF16),
             pltpu.VMEM(page_table.shape, jnp.int32),
             pltpu.SMEM(lengths.shape, jnp.int32),
-            pltpu.SMEM((pages,), jnp.int32),
-            pltpu.SMEM((pages,), jnp.int32),
+            pltpu.SMEM((pages + 1,), jnp.int32),
+            pltpu.SMEM((pages + 1,), jnp.int32),
+            pltpu.SMEM((pages + 1,), jnp.int32),
             pltpu.SemaphoreType.DMA((3,)),
         ],
         compiler_params=pltpu.CompilerParams(vmem_limit_bytes=20 << 20),

time: 153 us -> 152 us (level)
    pallas_call x1, Pallas kernels: 67.6 us -> 65.1 us  [finish(): pl.pallas_call(functools.partial(finish_kernel, Z), name='finish', out_sh...]
where the time goes in v4:
time: 152 us; the launch traced here: 149 us
  Pallas kernels  146 us (96%)
    pallas_call x1, Pallas kernels, project(): pl.pallas_call(functools.partial(project_kernel, Z), name='project', out_...  65.8 us
    pallas_call x1, Pallas kernels, finish(): pl.pallas_call(functools.partial(finish_kernel, Z), name='finish', out_sh...  65.1 us
    pallas_call x1, Pallas kernels, attend(): pl.pallas_call(attend_kernel, name='attend', out_shape=(jax.ShapeDtypeStr...  15.1 us

profile of v4, /device:TPU:33, one launch (start us, length us, event | category | flops | bytes accessed | tf_op | source)
XLA Modules:
  0.0 149.1 jit_solution(6780785950316629453)
XLA Ops:
  0.6 0.0 copy-start
  0.6 0.8 broadcast_add_fusion
  1.4 0.1 add_convert_fusion
  1.5 0.2 multiply_sine_fusion
  1.8 0.1 pad_maximum_fusion
  1.9 65.8 %project.1 = (bf16[8,32,16,384]{3,2,1,0:T(8,128)(2,1)S(1)}, bf16[128,384]{1,0:T(8,128)(2,1)S(1)}, bf16[128,384]{1,0:T(8,128)(2,1)S(1)}) custom-call(bf16[8,8,5120]{2,1,0:T(8,128)(2,1)} %x_hbm.1, bf16[8,8,5120]{2,1,0:T(8,128)(2,1)} %a_hbm.1, s32[8,8]{1,0:T(8,128)} %mask_hbm.1, f32[1,5120]{1,0:T(1,128)} %bitcast.18, f32[128,128]{1,0:T(8,128)S(1)} %get-tuple-element.14.cos_ref, ...), custom_call_target="tpu_custom_call" | custom-call | tf_op jit(solution)/shard_map/project/pallas_call | solution.py:385
  67.6 0.0 copy-done
  67.6 15.1 %attend.1 = (bf16[8,512,384]{2,1,0:T(8,128)(2,1)S(1)}, f32[512,128]{1,0:T(8,128)S(1)}) custom-call(s32[1]{0:T(128)} %bitcast.base, s32[8]{0:T(128)} %lengths_hbm.1, s32[4,128]{1,0:T(4,128)} %bitcast.19, bf16[8,512,384]{2,1,0:T(8,128)(2,1)S(1)} %bitcast.11, bf16[16,128,384]{2,1,0:T(8,128)(2,1)S(1)} %copy-done, bf16[16,128,384]{2,1,0:T(8,128)(2,1)} %v_hbm.1, ...), custom_call_target="tpu_custom_call" | custom-call | tf_op jit(solution)/shard_map/attend/pallas_call | solution.py:550
  82.8 65.1 %finish.1 = (bf16[8,8,640]{2,1,0:T(8,128)(2,1)S(1)}, bf16[8,8,640]{2,1,0:T(8,128)(2,1)S(1)}) custom-call(bf16[8,8,4,16,384]{4,3,2,1,0:T(8,128)(2,1)S(1)} %bitcast.12, f32[8,4,16,128]{3,2,1,0:T(8,128)S(1)} %bitcast.13, bf16[160,384]{1,0:T(8,128)(2,1)} %wo_ref.1), custom_call_target="tpu_custom_call" | custom-call | tf_op jit(solution)/shard_map/finish/pallas_call | solution.py:942
  147.9 0.6 copy.16
  148.5 0.6 copy.17
  (4 shorter events, 0.0 us)
Async XLA Ops:
  0.6 67.0 %copy-start = (bf16[16,128,384]{2,1,0:T(8,128)(2,1)S(1)}, bf16[16,128,384]{2,1,0:T(8,128)(2,1)}, u32[]{:S(2)}) copy-start(bf16[16,128,384]{2,1,0:T(8,128)(2,1)} %k_ref.1) | copy-start | bytes 4718596

commit v5 on v4

--- a/solution.py
+++ b/solution.py
@@ -34,10 +34,9 @@
 ORDER = (
     "q1", "q2", "k0", "tf", "q3", "k1", "v0", "th", "mq07", "q4", "mq78", "sq",
     "k2", "v1", "mk05", "cq", "p0", "k3", "v2", "rx", "p1", "p2", "k4", "mk58",
-    "sk", "v3", "p3", "p4", "v4", "mv08", "sv", "p5", "p6", "p7", "p8", "p9",
-    "ck", "cv",
+    "sk", "v3", "p3", "jk", "p4", "v4", "mv08", "sv", "p5", "p6", "jv", "p7",
+    "p8", "p9", "ck", "cv",
 )
-
 
 LATE = ("x16", "c0", "x68", "own", "wo", "m0", "c1", "m1", "y0", "y1")
 
@@ -216,6 +215,32 @@
             part[t, d - 1] = acc[t, pl.ds(pl.multiple_of(there * 128, 128), 128), :].astype(BF16)
             piece(t, d).start()
 
+    def rows_at(n):
+        return pl.ds(pl.multiple_of(lax.rem(x + n + X, X) * 128, 128), 128)
+
+    def relay(t, kind):
+        way = 1 if t == 1 else -1
+        target = at(0, X - way) if kind == 0 else at(0, X + way)
+        return remote(part.at[t, kind], got.at[t, kind], part_send.at[t, kind], part_recv.at[t, kind], target)
+
+    def spread_two(t):
+        way = 1 if t == 1 else -1
+        part[t, 1] = acc[t, rows_at(2), :].astype(BF16)
+        relay(t, 1).start()
+        part[t, 0] = acc[t, rows_at(-way), :].astype(BF16)
+        relay(t, 0).start()
+
+    def join_two(t):
+        way = 1 if t == 1 else -1
+        relay(t, 1).wait_recv()
+        part[t, 2] = (acc[t, rows_at(way), :] + got[t, 1].astype(F32)).astype(BF16)
+        relay(t, 2).start()
+
+    def collect_two(t):
+        relay(t, 0).wait_recv()
+        relay(t, 2).wait_recv()
+        return acc[t, mine, :] + got[t, 0].astype(F32) + got[t, 2].astype(F32)
+
     def collect(t):
         total = acc[t, mine, :]
         for d in range(1, X):
@@ -323,10 +348,10 @@
             rest_x(d).wait_recv()
 
     def key_ready():
-        kn_ref[...] = turn(collect(1))
+        kn_ref[...] = turn(collect_two(1))
 
     def value_ready():
-        vn_ref[...] = collect(2).astype(BF16)
+        vn_ref[...] = collect_two(2).astype(BF16)
 
     named = {
         "tf": forward_tokens,
@@ -341,8 +366,12 @@
             named[word]()
         elif word[0] == "m":
             multiply("qkv".index(word[1]), int(word[2]), int(word[3]))
+        elif word == "sq":
+            spread(0)
         elif word[0] == "s":
-            spread("qkv".index(word[1]))
+            spread_two("qkv".index(word[1]))
+        elif word[0] == "j":
+            join_two("qkv".index(word[1]))
         elif word[0] == "p":
             pass_on(int(word[1]), int(word[1]) + 1)
         else:
@@ -356,7 +385,7 @@
                 for bit in range(PARTS):
                     ring(right, t, k, bit).wait_send()
         for d in range(1, X):
-            piece(t, d).wait_send()
+            (piece(t, d) if t == 0 else relay(t, d - 1)).wait_send()
     for d in range(1, X):
         token(d).wait_send()
     for d in range(X):
@@ -532,12 +561,15 @@
         for j in range(PAIR):
             page_part(i * PAIR + j)
 
-    @pl.loop(0, q_ref.shape[0])
-    def _(r):
-        for h in range(heads):
-            o_ref[r, :, h * HD : (h + 1) * HD] = jnp.transpose(acc[r, h].astype(BF16))
-
-    st_ref[...] = jnp.transpose(stats[...])
+    @pl.loop(0, q_ref.shape[0] // UNROLL)
+    def _(i):
+        for j in range(UNROLL):
+            r = i * UNROLL + j
+            for h in range(heads):
+                o_ref[r, :, h * HD : (h + 1) * HD] = jnp.transpose(acc[r, h].astype(BF16))
+
+    rows = jnp.transpose(stats[...]).reshape(queries // 16, 16, 128)
+    st_ref[...] = rows[:, :8] + pltpu.roll(rows[:, 8:], 64, 2)
 
 
 def attend(base, lengths, page_table, q_all, key_cache, value_cache, new_keys, new_values):
@@ -552,7 +584,7 @@
         name="attend",
         out_shape=(
             jax.ShapeDtypeStruct((requests, queries, cols), BF16),
-            jax.ShapeDtypeStruct((queries, 128), F32),
+            jax.ShapeDtypeStruct((queries // 16, 8, 128), F32),
         ),
         in_specs=[smem, hbm, hbm, vmem, vmem, hbm, vmem, vmem],
         out_specs=(vmem, vmem),
@@ -580,10 +612,14 @@
     return jnp.where(lax.rem(lane, 8) >= 4, total, peak), factors
 
 
+def per_row(table, lane):
+    return jnp.concatenate([table[:, lane : lane + 1], table[:, lane + 64 : lane + 65]], axis=0)
+
+
 def weigh(factors, sources, r, h):
     lane = r * 8 + h
     return sum(
-        factor[:, lane : lane + 1] * source[:, h * HD : (h + 1) * HD].astype(F32)
+        per_row(factor, lane) * source[:, h * HD : (h + 1) * HD].astype(F32)
         for factor, source in zip(factors, sources)
     )
 
@@ -824,7 +860,7 @@
             sources = [cb[half, z, r]] + [rb[half, i, r] for i in range(Z - 1)]
             for h in range(heads):
                 lane = (half * span + r) * 8 + h
-                value = weigh(factors, sources, half * span + r, h) * inverse[:, lane + 4 : lane + 5]
+                value = weigh(factors, sources, half * span + r, h) * per_row(inverse, lane + 4)
                 ctx[half, pl.ds(mine + r * 16, 16), h * HD : (h + 1) * HD] = value.astype(BF16)
         for d in (2, 1, 3):
             share(half, d).start()
@@ -938,7 +974,7 @@
     dma = pltpu.SemaphoreType.DMA
     shape = jax.ShapeDtypeStruct((requests, tokens, X * BLK), BF16)
     chunks = pltpu.VMEM((2, Z, requests // 2, 16, cols), BF16)
-    tables = pltpu.VMEM((Z, 16, 128), F32)
+    tables = pltpu.VMEM((Z, 8, 128), F32)
     return pl.pallas_call(
         functools.partial(finish_kernel, Z),
         name="finish",
@@ -957,7 +993,7 @@
             chunks,
             tables,
             pltpu.VMEM((2, Z - 1, requests // 2, 16, cols), BF16),
-            pltpu.VMEM((Z - 1, 16, 128), F32),
+            pltpu.VMEM((Z - 1, 8, 128), F32),
             pltpu.VMEM((ys, 2, BLK, cols), BF16),
             pltpu.VMEM((2, X * rows // 2, cols), BF16),
             pltpu.VMEM((2, ys, BLK, X * rows // 2), BF16),
@@ -1045,7 +1081,7 @@
         new_keys.reshape(requests, 16, cols),
         new_values.reshape(requests, 16, cols),
     )
-    return finish(Z, out.reshape(requests, Z, X, 16, cols), table.reshape(Z, X, 16, 128), w_out, tokens)
+    return finish(Z, out.reshape(requests, Z, X, 16, cols), table.reshape(Z, X, 8, 128), w_out, tokens)
 
 
 def solution(mesh):

time: 152 us -> 150 us (0.987)
    pallas_call x1, Pallas kernels: 65.1 us -> 68.1 us  [finish(): pl.pallas_call(functools.partial(finish_kernel, Z), name='finish', out_sh...]
    pallas_call x1, Pallas kernels: 65.8 us -> 63.8 us  [project(): pl.pallas_call(functools.partial(project_kernel, Z), name='project', out_...]
    pallas_call x1, Pallas kernels: 15.1 us -> 13.2 us  [attend(): pl.pallas_call(attend_kernel, name='attend', out_shape=(jax.ShapeDtypeStr...]
where the time goes in v5:
time: 150 us; the launch traced here: 148 us
  Pallas kernels  145 us (97%)
    pallas_call x1, Pallas kernels, finish(): pl.pallas_call(functools.partial(finish_kernel, Z), name='finish', out_sh...  68.1 us
    pallas_call x1, Pallas kernels, project(): pl.pallas_call(functools.partial(project_kernel, Z), name='project', out_...  63.8 us
    pallas_call x1, Pallas kernels, attend(): pl.pallas_call(attend_kernel, name='attend', out_shape=(jax.ShapeDtypeStr...  13.2 us

profile of v5, /device:TPU:33, one launch (start us, length us, event | category | flops | bytes accessed | tf_op | source)
XLA Modules:
  0.0 148.2 jit_solution(6511356848717904923)
XLA Ops:
  0.6 0.0 copy-start
  0.6 0.8 broadcast_add_fusion
  1.4 0.1 add_convert_fusion
  1.5 0.2 multiply_sine_fusion
  1.8 0.1 pad_maximum_fusion
  1.9 63.8 %project.1 = (bf16[8,32,16,384]{3,2,1,0:T(8,128)(2,1)S(1)}, bf16[128,384]{1,0:T(8,128)(2,1)S(1)}, bf16[128,384]{1,0:T(8,128)(2,1)S(1)}) custom-call(bf16[8,8,5120]{2,1,0:T(8,128)(2,1)} %x_hbm.1, bf16[8,8,5120]{2,1,0:T(8,128)(2,1)} %a_hbm.1, s32[8,8]{1,0:T(8,128)} %mask_hbm.1, f32[1,5120]{1,0:T(1,128)} %bitcast.18, f32[128,128]{1,0:T(8,128)S(1)} %get-tuple-element.14.cos_ref, ...), custom_call_target="tpu_custom_call" | custom-call | tf_op jit(solution)/shard_map/project/pallas_call | solution.py:414
  65.7 0.0 copy-done
  65.7 13.2 %attend.1 = (bf16[8,512,384]{2,1,0:T(8,128)(2,1)S(1)}, f32[32,8,128]{2,1,0:T(8,128)S(1)}) custom-call(s32[1]{0:T(128)} %bitcast.base, s32[8]{0:T(128)} %lengths_hbm.1, s32[4,128]{1,0:T(4,128)} %bitcast.19, bf16[8,512,384]{2,1,0:T(8,128)(2,1)S(1)} %bitcast.11, bf16[16,128,384]{2,1,0:T(8,128)(2,1)S(1)} %copy-done, bf16[16,128,384]{2,1,0:T(8,128)(2,1)} %v_hbm.1, ...), custom_call_target="tpu_custom_call" | custom-call | tf_op jit(solution)/shard_map/attend/pallas_call | solution.py:582
  78.8 68.1 %finish.1 = (bf16[8,8,640]{2,1,0:T(8,128)(2,1)S(1)}, bf16[8,8,640]{2,1,0:T(8,128)(2,1)S(1)}) custom-call(bf16[8,8,4,16,384]{4,3,2,1,0:T(8,128)(2,1)S(1)} %bitcast.12, f32[8,4,8,128]{3,2,1,0:T(8,128)S(1)} %bitcast.13, bf16[160,384]{1,0:T(8,128)(2,1)} %wo_ref.1), custom_call_target="tpu_custom_call" | custom-call | tf_op jit(solution)/shard_map/finish/pallas_call | solution.py:978
  147.0 0.6 copy.16
  147.6 0.6 copy.17
  (4 shorter events, 0.0 us)
Async XLA Ops:
  0.6 65.0 %copy-start = (bf16[16,128,384]{2,1,0:T(8,128)(2,1)S(1)}, bf16[16,128,384]{2,1,0:T(8,128)(2,1)}, u32[]{:S(2)}) copy-start(bf16[16,128,384]{2,1,0:T(8,128)(2,1)} %k_ref.1) | copy-start | bytes 4718596
